TPU v7x, 128 devices: a whole 4x4x4 slice. The times are simulated.
128 devices in a mesh: mem: 8 (over y_hi, x), dom: 16 (over z, y_lo, core).
Axes of the slice: x: 4, y: 4 (y_hi: 2, y_lo: 2; y = y_hi * 2 + y_lo), z: 4, core: 2. Of those that a mesh axis runs over, the one named last changes fastest.
Arguments:
- sample_vectors_prior: float32 [32, 5, 512, 256], P('mem', None, 'dom'), may hold values from -6 to 6
- smoothing_number: float32 [5, 512, 256], P(None, 'dom'), may hold values from 0.02 to 0.2
- cross_quantity_factor: float32 [5, 5], replicated, may hold values from -0.6 to 0.6
- obs_tile: int32 [2, 2048, 1], replicated, may hold values from 0 to 15; in each aligned block of 2048 rows (0 to 2047, 2048 to 4095, ..., all dimensions but the last counted through in order) at most 256 rows name the same one
- measured_gridpoint: int32 [2, 2048], replicated, may hold values from 0 to 7904
- obs_field: int32 [2, 2048], replicated, may hold values from 0 to 4
- obs_weights: float32 [2, 2048, 4], replicated, may hold values from 0.1 to 0.5
- obs_values: float32 [2, 2048], replicated, may hold values from -8 to 8
- observation_variance: float32 [2, 2048], replicated, may hold values from 0.2 to 2
- localization: float32 [2, 16, 2048], P(None, 'dom'), may hold values from 0.001 to 0.02
Outputs:
- analysis: float32 [32, 5, 512, 256], P('mem', None, 'dom')
Inputs may be any that keep to these rules, and one draw needn't show every extreme that they name: `obs_tile`: in each batch at most 256 observations share an owning tile, and in some batch some tile owns exactly 256. Local row measured_gridpoint // 255, column measured_gridpoint % 255; the four points used lie in the owning tile.
All inputs are finite; a program needn't handle non-finite values.
Results may differ from a plain program's by a relative error of at most 0.0001.
Values sent between devices are 32-bit elements; how exact they have to be, the bound alone decides.
No kernel may reach another device: no remote copies, remote signals or barrier semaphores. Data moves between devices by JAX's collectives and lax.ppermute only.
A program may use at most 128 MiB of HBM per device.

v0:
```python
import jax
import jax.numpy as jnp
from jax import lax
from jax.sharding import PartitionSpec as P

STEPS = 2


def with_halo(cells, sides, width):
    for axis, dim in sides:
        count = lax.axis_size(axis)
        ends = count - 1
        head = lax.slice_in_dim(cells, 0, width, axis=dim)
        tail = lax.slice_in_dim(cells, cells.shape[dim] - width, cells.shape[dim], axis=dim)
        cells = jnp.concatenate(
            [
                lax.ppermute(tail, axis, [(i, (i + 1) % count) for i in range(ends)]),
                cells,
                lax.ppermute(head, axis, [((i + 1) % count, i) for i in range(ends)]),
            ],
            axis=dim,
        )
    return cells


def predicted_quantity(sample_vectors_prior, smoothing_number, cross_quantity_factor):
    padded = with_halo(sample_vectors_prior, (("dom", 2),), 1)
    padded = jnp.pad(padded, ((0, 0), (0, 0), (0, 0), (1, 1)))
    lap = padded[:, :, 2:, 1:-1] + padded[:, :, :-2, 1:-1]
    lap = lap + padded[:, :, 1:-1, 2:] + padded[:, :, 1:-1, :-2] - 4.0 * sample_vectors_prior
    mixed = jnp.einsum(
        "fg,mgxy->mfxy",
        cross_quantity_factor,
        sample_vectors_prior,
        precision=lax.Precision.HIGHEST,
    )
    return sample_vectors_prior + smoothing_number[None] * lap + mixed


def local_priors(
    sample_vectors_prior, obs_tile, measured_gridpoint, obs_field, obs_weights, batch_index, my_tile
):
    sample_total_size, fields, tile_row_count, columns = sample_vectors_prior.shape
    nobs_count = measured_gridpoint.shape[1]
    offsets = jnp.array([0, 1, columns, columns + 1], dtype=jnp.int32)
    owner = obs_tile[batch_index, :, 0]
    place = measured_gridpoint[batch_index]
    base = (
        obs_field[batch_index] * (tile_row_count * columns)
        + place // (columns - 1) * columns
        + place % (columns - 1)
    )
    points = (base[:, None] + offsets[None, :]).reshape(-1)
    flat = sample_vectors_prior.reshape(sample_total_size, fields * tile_row_count * columns)
    values = jnp.take(flat, points, axis=1).reshape(sample_total_size, nobs_count, 4)
    local_prior = jnp.sum(values * obs_weights[batch_index][None], axis=-1)
    owned_mask = owner == my_tile
    return (local_prior, owner, owned_mask)


def share_priors(local_prior, owned_mask):
    masked = jnp.where(owned_mask[None], local_prior, jnp.float32(0.0))
    summed = lax.psum(masked, "dom")
    prior = lax.all_gather(summed, "mem", axis=0, tiled=True)
    return prior


def batch_mixing(prior, obs_values, observation_variance, localization, batch_index):
    members = prior.shape[0]
    mean_prior = jnp.mean(prior, axis=0)
    ensemble_spread = prior - mean_prior[None]
    variance = jnp.sum(ensemble_spread * ensemble_spread, axis=0) / (members - 1)
    error = observation_variance[batch_index]
    total = variance + error
    gain = (obs_values[batch_index] - mean_prior)[None] / total[None] - ensemble_spread / (
        jnp.sqrt(total) * (jnp.sqrt(error) + jnp.sqrt(total))
    )[None]
    return jnp.einsum(
        "mo,to,no->tmn",
        ensemble_spread,
        localization[batch_index],
        gain,
        precision=lax.Precision.HIGHEST,
    )[0] / (members - 1)


def apply_update(sample_vectors_prior, mixing):
    sample_total_size, fields, tile_row_count, columns = sample_vectors_prior.shape
    members = sample_total_size * lax.axis_size("mem")
    flat = sample_vectors_prior.reshape(sample_total_size, fields * tile_row_count * columns)
    own_columns = lax.dynamic_slice_in_dim(
        mixing, lax.axis_index("mem") * sample_total_size, sample_total_size, 1
    )
    piece = lax.all_gather(flat, "mem", axis=0, tiled=True)
    product = jnp.dot(
        own_columns.T, piece, precision=lax.Precision.HIGHEST, preferred_element_type=jnp.float32
    )
    member_total = jnp.sum(piece, axis=0)
    average = member_total / members
    updated = flat + product - jnp.sum(own_columns, axis=0)[:, None] * average[None]
    return updated.reshape(sample_total_size, fields, tile_row_count, columns)


def on_device(
    sample_vectors_prior,
    smoothing_number,
    cross_quantity_factor,
    obs_tile,
    measured_gridpoint,
    obs_field,
    obs_weights,
    obs_values,
    observation_variance,
    localization,
):
    my_tile = lax.axis_index("dom")
    for step_index in range(STEPS):
        sample_vectors_prior = predicted_quantity(
            sample_vectors_prior, smoothing_number, cross_quantity_factor
        )
    batch_count = obs_values.shape[0]
    for batch_index in range(batch_count):
        local_prior, owner, owned_mask = local_priors(
            sample_vectors_prior,
            obs_tile,
            measured_gridpoint,
            obs_field,
            obs_weights,
            batch_index,
            my_tile,
        )
        prior = share_priors(local_prior, owned_mask)
        mixing = batch_mixing(prior, obs_values, observation_variance, localization, batch_index)
        sample_vectors_prior = apply_update(sample_vectors_prior, mixing)
    return sample_vectors_prior


def solution(mesh):
    placed = (
        P("mem", None, "dom", None),
        P(None, "dom", None),
        P(),
        P(),
        P(),
        P(),
        P(),
        P(),
        P(),
        P(None, "dom", None),
    )
    return jax.shard_map(
        on_device,
        mesh=mesh,
        in_specs=placed,
        out_specs=P("mem", None, "dom", None),
        check_vma=False,
    )
```

profile of v0, /device:TPU:0, one launch (start us, length us, event | category | flops | bytes accessed | tf_op | source)
XLA Modules:
  0.0 404.2 jit_solution(9559365138855716027)
XLA Ops:
  6.5 1.5 copy.48
  9.4 3.0 collective-permute-start.1
  14.0 1.4 fusion.4
  16.6 3.8 collective-permute-start.3
  21.8 1.4 fusion.3
  27.1 10.0 %copy.51 = f32[4,40960]{0,1:T(8,128)} copy(f32[4,40960]{1,0:T(4,128)S(1)} %bitcast.60) | data formatting | bytes 1310720 | tf_op jit(solution)/shard_map/reshape | solution.py:90
  37.1 35.3 %gather_fusion = f32[8192,4]{1,0:T(8,128)} fusion(f32[4,40960]{0,1:T(8,128)} %copy.51, s32[8192]{0:T(1024)S(1)} %fusion.31), kind=kCustom, calls=%fused_computation.clone | custom fusion | bytes 294912 | tf_op jit(solution)/shard_map/jit(_take)/gather | solution.py:55
  72.4 6.2 %broadcast_select_fusion.1 = f32[8192,4]{1,0:T(8,128)S(1)} fusion(f32[8192,4]{1,0:T(8,128)} %gather_fusion, pred[8192]{0:T(1024)(128)(4,1)S(1)} %compare_and_fusion.1), kind=kLoop, calls=%fused_computation.11 | loop fusion | flops 32768 | bytes 270336 | tf_op jit(solution)/shard_map/jit(_take)/select_n | solution.py:55
  78.6 11.2 %multiply_reduce_fusion.1 = f32[4,2048]{0,1:T(8,128)S(1)} fusion(f32[4,2048,4]{0,2,1:T(4,128)S(1)} %bitcast.56, f32[2048,4]{1,0:T(8,128)S(1)} %copy.52), kind=kLoop, calls=%fused_computation.7 | loop fusion | flops 57344 | bytes 196608 | tf_op jit(solution)/shard_map/reduce_sum | solution.py:56
  90.2 72.1 %psum.14 = f32[4,2048]{0,1:T(8,128)} all-reduce(f32[4,2048]{0,1:T(8,128)S(1)} %broadcast_select_fusion.3), channel_id=1, replica_groups=mesh['mem'=8,'dom'=16] {'dom'}, use_global_device_ids=true, to_apply=%region_1.3 | all-reduce | flops 8192 | bytes 65536 | tf_op jit(solution)/shard_map/psum | solution.py:63
  162.3 1.6 copy.53
  163.9 35.0 %all-gather = f32[8,4,2048]{2,1,0:T(4,128)S(1)} all-gather(f32[1,4,2048]{2,1,0:T(4,128)S(1)} %copy.53), channel_id=1, replica_groups=mesh['mem'=8,'dom'=16] {'mem'}, dimensions={0}, use_global_device_ids=true | all-gather | bytes 294912 | tf_op jit(solution)/shard_map/all_gather | solution.py:64
  199.7 3.5 reduce_sum.94
  203.2 6.0 %reshape.218 = f32[32,40960]{1,0:T(8,128)} reshape(f32[8,4,40960]{2,1,0:T(4,128)} %all-gather.7.cloned.1.call-done) | data formatting | bytes 10485760
  209.2 6.0 %fusion.1 = f32[4,40960]{1,0:T(4,128)} fusion(f32[4,40960]{1,0:T(4,128)S(1)} %bitcast.61, f32[32,40960]{1,0:T(8,128)} %reshape.218, f32[40960]{0:T(1024)S(1)} %broadcast_multiply_fusion.1, f32[4]{0:T(128)S(1)} %fusion.41, f32[32,32]{0,1:T(8,128)S(1)} %fusion.17, s32[]{:T(128)S(6)} %select_n.56), kind=kOutput, calls=%fused_computation.5 | convolution fusion | flops 63406208 | bytes 6720004 | tf_op jit(solution)/shard_map/dot_general | solution.py:95
  216.2 11.0 %copy.55 = f32[4,40960]{0,1:T(8,128)} copy(f32[4,40960]{1,0:T(4,128)} %fusion.1) | data formatting | bytes 1310720 | tf_op jit(solution)/shard_map/sub | solution.py:100
  227.2 34.7 %gather_fusion.1 = f32[8192,4]{1,0:T(8,128)} fusion(f32[4,40960]{0,1:T(8,128)} %copy.55, s32[8192]{0:T(1024)S(1)} %fusion.32), kind=kCustom, calls=%fused_computation.1.clone | custom fusion | bytes 294912 | tf_op jit(solution)/shard_map/jit(_take)/gather | solution.py:55
  261.9 6.2 %broadcast_select_fusion = f32[8192,4]{1,0:T(8,128)S(1)} fusion(f32[8192,4]{1,0:T(8,128)} %gather_fusion.1, pred[8192]{0:T(1024)(128)(4,1)S(1)} %compare_and_fusion), kind=kLoop, calls=%fused_computation.10 | loop fusion | flops 32768 | bytes 270336 | tf_op jit(solution)/shard_map/jit(_take)/select_n | solution.py:55
  268.2 11.2 %multiply_reduce_fusion = f32[4,2048]{0,1:T(8,128)S(1)} fusion(f32[4,2048,4]{0,2,1:T(4,128)S(1)} %bitcast.57, f32[2048,4]{1,0:T(8,128)S(1)} %copy.56), kind=kLoop, calls=%fused_computation.6 | loop fusion | flops 57344 | bytes 196608 | tf_op jit(solution)/shard_map/reduce_sum | solution.py:56
  279.7 66.1 %psum.15 = f32[4,2048]{0,1:T(8,128)S(1)} all-reduce(f32[4,2048]{0,1:T(8,128)S(1)} %broadcast_select_fusion.2), channel_id=1, replica_groups=mesh['mem'=8,'dom'=16] {'dom'}, use_global_device_ids=true, to_apply=%region_7.9 | all-reduce | flops 8192 | bytes 65536 | tf_op jit(solution)/shard_map/psum | solution.py:63
  346.2 34.7 %all-gather.2 = f32[8,4,2048]{2,1,0:T(4,128)S(1)} all-gather(f32[1,4,2048]{2,1,0:T(4,128)S(1)} %copy.57), channel_id=1, replica_groups=mesh['mem'=8,'dom'=16] {'mem'}, dimensions={0}, use_global_device_ids=true | all-gather | bytes 294912 | tf_op jit(solution)/shard_map/all_gather | solution.py:64
  381.7 3.5 reduce_sum.99
  385.2 6.1 %reshape.222 = f32[32,40960]{1,0:T(8,128)} reshape(f32[8,4,40960]{2,1,0:T(4,128)} %all-gather.9.cloned.1.call-done) | data formatting | bytes 10485760
  391.3 5.1 %fusion = f32[4,40960]{1,0:T(4,128)S(1)} fusion(f32[4,40960]{1,0:T(4,128)S(1)} %copy-done.2, f32[32,40960]{1,0:T(8,128)} %reshape.222, f32[40960]{0:T(1024)S(1)} %broadcast_multiply_fusion, f32[4]{0:T(128)S(1)} %fusion.42, f32[32,32]{0,1:T(8,128)S(1)} %fusion.13, s32[]{:T(128)S(6)} %select_n.56), kind=kOutput, calls=%fused_computation.3 | convolution fusion | flops 63406208 | bytes 6720004 | tf_op jit(solution)/shard_map/dot_general | solution.py:95
  (80 shorter events, 13.8 us)
Async XLA Ops:
  6.5 7.4 %copy-start = (f32[5,5]{1,0:T(8,128)S(1)}, f32[5,5]{1,0:T(8,128)}, u32[]{:S(2)}) copy-start(f32[5,5]{1,0:T(8,128)} %param.16) | copy-start | bytes 304
  6.5 193.1 %all-gather.7.cloned.1.call-start = ((), (), s32[]{:S(2)}) async-start(), calls=%async_computation | async-start | bytes 5898240 | tf_op jit(solution)/shard_map/all_gather | solution.py:94
  8.1 5.4 %collective-permute-start = (f32[4,5,1,256]{3,1,2,0:T(8,128)S(1)}, f32[4,5,1,256]{3,1,2,0:T(8,128)S(1)}, u32[]{:S(2)}, u32[]{:S(2)}) collective-permute-start(f32[4,5,1,256]{3,1,2,0:T(8,128)S(1)} %get-tuple-element.13), channel_id=1, source_target_pairs={{1,0},{2,1},{3,2},{4,3},{5,4},{6,5},{7,6},{8,7},{9,8},{10,9},{11,1... | collective-permute-start | bytes 61448 | tf_op jit(solution)/shard_map/ppermute | solution.py:19
  9.4 4.1 %collective-permute-start.1 = (f32[4,5,1,256]{3,1,2,0:T(8,128)S(1)}, f32[4,5,1,256]{3,1,2,0:T(8,128)S(1)}, u32[]{:S(2)}, u32[]{:S(2)}) collective-permute-start(f32[4,5,1,256]{3,1,2,0:T(8,128)S(1)} %get-tuple-element.12), channel_id=1, source_target_pairs={{0,1},{1,2},{2,3},{3,4},{4,5},{5,6},{6,7},{7,8},{8,9},{9,10},{10,1... | collective-permute-start | bytes 61448 | tf_op jit(solution)/shard_map/ppermute | solution.py:17
  15.3 5.1 %collective-permute-start.2 = (f32[4,5,1,256]{3,1,2,0:T(8,128)S(1)}, f32[4,5,1,256]{3,1,2,0:T(8,128)S(1)}, u32[]{:S(2)}, u32[]{:S(2)}) collective-permute-start(f32[4,5,1,256]{3,1,2,0:T(8,128)S(1)} %get-tuple-element.11), channel_id=1, source_target_pairs={{1,0},{2,1},{3,2},{4,3},{5,4},{6,5},{7,6},{8,7},{9,8},{10,9},{11,1... | collective-permute-start | bytes 61448 | tf_op jit(solution)/shard_map/ppermute | solution.py:19
  16.6 4.7 %collective-permute-start.3 = (f32[4,5,1,256]{3,1,2,0:T(8,128)S(1)}, f32[4,5,1,256]{3,1,2,0:T(8,128)S(1)}, u32[]{:S(2)}, u32[]{:S(2)}) collective-permute-start(f32[4,5,1,256]{3,1,2,0:T(8,128)S(1)} %get-tuple-element.10), channel_id=1, source_target_pairs={{0,1},{1,2},{2,3},{3,4},{4,5},{5,6},{6,7},{7,8},{8,9},{9,10},{10,1... | collective-permute-start | bytes 61448 | tf_op jit(solution)/shard_map/ppermute | solution.py:17
  21.8 2.9 copy-start.3
  21.8 3.0 copy-start.5
  21.8 3.1 copy-start.10
  23.2 3.0 copy-start.4
  23.2 3.3 copy-start.6
  23.2 3.4 copy-start.7
  24.6 357.1 %all-gather.9.cloned.1.call-start = ((), (), s32[]{:S(2)}) async-start(), calls=%async_computation.1 | async-start | bytes 5898240 | tf_op jit(solution)/shard_map/all_gather | solution.py:94
  89.8 109.3 %copy-start.8 = (f32[2,2048]{1,0:T(2,128)S(1)}, f32[2,2048]{1,0:T(2,128)}, u32[]{:S(2)}) copy-start(f32[2,2048]{1,0:T(2,128)} %param.21) | copy-start | bytes 49156
  89.8 109.3 %copy-start.9 = (f32[2,2048]{1,0:T(2,128)S(1)}, f32[2,2048]{1,0:T(2,128)}, u32[]{:S(2)}) copy-start(f32[2,2048]{1,0:T(2,128)} %param.22) | copy-start | bytes 49156
  385.2 6.1 %copy-start.2 = (f32[4,40960]{1,0:T(4,128)S(1)}, f32[4,40960]{1,0:T(4,128)}, u32[]{:S(2)}) copy-start(f32[4,40960]{1,0:T(4,128)} %fusion.1) | copy-start | bytes 1966084
  385.2 12.2 %copy-start.1 = (f32[5,5]{1,0:T(8,128)S(1)}, f32[5,5]{1,0:T(8,128)}, u32[]{:S(2)}) copy-start(f32[5,5]{1,0:T(8,128)} %param.16) | copy-start | bytes 304
Sparse Core Ops, SparseCore 0:
  24.8 87.9 all-gather.6
  215.3 78.2 all-gather.8
where the time goes:
time: 405 us; the launch traced here: 404 us
  blocking collectives  208 us (51%)
  local copies, waits for them, and re-layouts  113 us (28%)
  other arithmetic  44.9 us (11%)
  matrix products  14.5 us (4%)
  between operations  13.9 us (3%)
  starting transfers between devices  9.47 us (2%)
    psum x2, blocking collectives, share_priors(): summed = lax.psum(masked, 'dom')  138 us
    gather x2, local copies, waits for them, and re-layouts, local_priors(): jnp.take(flat, points, axis=1).reshape(sample_total_size, nobs_count, 4)  70 us
    all_gather x2, blocking collectives, share_priors(): prior = lax.all_gather(summed, 'mem', axis=0, tiled=True)  69.7 us
    reduce_sum x2, other arithmetic, local_priors(): local_prior = jnp.sum(values * obs_weights[batch_index][None], axis=-1)  22.4 us
    unnamed x33, local copies, waits for them, and re-layouts  19.3 us
    select_n x2, other arithmetic, local_priors(): jnp.take(flat, points, axis=1).reshape(sample_total_size, nobs_count, 4)  12.4 us
    dot_general x2, matrix products, apply_update(): jnp.dot(own_columns.T, piece, precision=lax.Precision.HIGHEST, preferred_...  11.1 us
    sub x1, local copies, waits for them, and re-layouts, apply_update(): flat + product - jnp.sum(own_columns, axis=0)[:, None] * average[None]  11 us
  transfers between devices with their start and end apart: 6, of which 1 were waited for; matrix products, arithmetic and copies ran while one was open for 33% of the time, Pallas kernels for 0%

commit v1 on v0

v1 whole, which is shorter than its diff:
```python
import jax
import jax.numpy as jnp
from jax import lax
from jax.experimental import pallas as pl
from jax.experimental.pallas import tpu as pltpu
from jax.sharding import PartitionSpec as P

F32 = jnp.float32
BF16 = jnp.bfloat16
HI = lax.Precision.HIGHEST
CAP = 256
LANES = 128


def split3(values):
    high = values.astype(BF16)
    rest = values - high.astype(F32)
    middle = rest.astype(BF16)
    low = (rest - middle.astype(F32)).astype(BF16)
    return high, middle, low


def dot_nt(a, b, precision=None):
    return lax.dot_general(
        a, b, (((1,), (1,)), ((), ())), precision=precision, preferred_element_type=F32
    )


def dot_nn(a, b, precision=None):
    return lax.dot_general(
        a, b, (((1,), (0,)), ((), ())), precision=precision, preferred_element_type=F32
    )


def iota(shape, dim):
    return lax.broadcasted_iota(jnp.int32, shape, dim)


def chosen_rows(slots, row):
    return jnp.where(slots[row : row + 1, :] == iota((CAP, LANES), 0), 1.0, 0.0).astype(BF16)


def compact_kernel(tile_ref, owner_ref, place_ref, field_ref, weight_ref, value_ref, error_ref,
                   params_ref, slots_ref, mask_ref, vals_ref):
    batches, _, count = owner_ref.shape
    chunks = count // LANES
    rows = batches * chunks
    mine = tile_ref[0]
    for b in range(batches):
        own = jnp.where(owner_ref[b] == mine, 1.0, 0.0)
        for j in range(chunks):
            mask_ref[b * chunks + j : b * chunks + j + 1, :] = own[:, j * LANES : (j + 1) * LANES]
    mask = mask_ref[...]
    mask16 = mask.astype(BF16)
    upper = jnp.where(iota((LANES, LANES), 0) <= iota((LANES, LANES), 1), 1.0, 0.0).astype(BF16)
    inside = dot_nn(mask16, upper)
    totals = dot_nn(mask16, jnp.ones((LANES, LANES), BF16)).astype(BF16)
    a, c = iota((rows, rows), 0), iota((rows, rows), 1)
    before = jnp.where((c < a) & ((c >= chunks) == (a >= chunks)), 1.0, 0.0).astype(BF16)
    rank = inside + dot_nn(before, totals) - 1.0
    slots = jnp.where(mask > 0.5, rank, -1.0).astype(jnp.int32)
    slots_ref[...] = slots
    for b in range(batches):
        place = place_ref[b : b + 1, :]
        row = ((place.astype(F32) + 0.5) * (1.0 / 255.0)).astype(jnp.int32)
        vals_ref[b, 0:1, :] = (field_ref[b : b + 1, :] * 32 + row).astype(F32)
        vals_ref[b, 1:2, :] = (place - row * 255).astype(F32)
        vals_ref[b, 2:6, :] = weight_ref[b]
        vals_ref[b, 6:7, :] = value_ref[b : b + 1, :]
        vals_ref[b, 7:8, :] = error_ref[b : b + 1, :]
        total = jnp.zeros((24, CAP), F32)
        for j in range(chunks):
            parts = split3(vals_ref[b, :, j * LANES : (j + 1) * LANES])
            total = total + dot_nt(
                jnp.concatenate([p.astype(F32) for p in parts], axis=0).astype(BF16),
                chosen_rows(slots, b * chunks + j),
            )
        params_ref[:, b * CAP : (b + 1) * CAP] = total[0:8] + total[8:16] + total[16:24]


def localize_kernel(slots_ref, loc_ref, out_ref):
    batches, tiles, count = loc_ref.shape
    chunks = count // LANES
    slots = slots_ref[...]
    for b in range(batches):
        total = jnp.zeros((3 * tiles, CAP), F32)
        for j in range(chunks):
            parts = split3(loc_ref[b, :, j * LANES : (j + 1) * LANES])
            total = total + dot_nt(
                jnp.concatenate(parts, axis=0), chosen_rows(slots, b * chunks + j)
            )
        out_ref[b] = total[:tiles] + total[tiles : 2 * tiles] + total[2 * tiles :]


TOP = 16


def forecast_kernel(cross_ref, x_ref, above_ref, below_ref, smooth_ref, params_ref,
                    out_ref, buf_ref, nxt_ref, sm_ref, fin_ref, u_ref):
    members, fields, nrows, cols = x_ref.shape
    last = TOP + nrows
    for f in range(fields):
        sm_ref[f, TOP - 1 : TOP, :] = above_ref[members, f, 1:2, :]
        sm_ref[f, TOP:last, :] = smooth_ref[f]
        sm_ref[f, last : last + 1, :] = below_ref[members, f, 0:1, :]
    for m in range(members):
        for f in range(fields):
            buf_ref[m * fields + f, TOP - 2 : TOP, :] = above_ref[m, f]
            buf_ref[m * fields + f, TOP:last, :] = x_ref[m, f]
            buf_ref[m * fields + f, last : last + 2, :] = below_ref[m, f]
    lane = iota((8, cols), 1)
    first_col, last_col = lane == 0, lane == cols - 1

    def substep(src_ref, m, base):
        own = [src_ref[m * fields + f, base : base + 8, :] for f in range(fields)]
        result = []
        for f in range(fields):
            v = own[f]
            lap = src_ref[m * fields + f, base + 1 : base + 9, :]
            lap = lap + src_ref[m * fields + f, base - 1 : base + 7, :]
            lap = lap + jnp.where(last_col, 0.0, pltpu.roll(v, cols - 1, 1))
            lap = lap + jnp.where(first_col, 0.0, pltpu.roll(v, 1, 1)) - 4.0 * v
            mixed = cross_ref[f, 0] * own[0]
            for g in range(1, fields):
                mixed = mixed + cross_ref[f, g] * own[g]
            result.append(v + sm_ref[f, base : base + 8, :] * lap + mixed)
        return result

    def member(m, carry):
        for base in range(TOP - 8, last + 8, 8):
            for f, v in enumerate(substep(buf_ref, m, base)):
                nxt_ref[m * fields + f, base : base + 8, :] = v
        for g in range(nrows // 8):
            for f, v in enumerate(substep(nxt_ref, m, TOP + 8 * g)):
                fin_ref[m, f * nrows + 8 * g : f * nrows + 8 * g + 8, :] = v
        return carry

    lax.fori_loop(0, members, member, 0)

    points = fields * nrows
    slots = params_ref.shape[1]
    spot = params_ref[0:1, :].astype(jnp.int32)
    column = params_ref[1:2, :].astype(jnp.int32)
    cid = iota((cols, slots), 0)
    left = jnp.where(cid == column, 1.0, 0.0).astype(BF16)
    right = jnp.where(cid == column + 1, 1.0, 0.0).astype(BF16)
    choice = jnp.concatenate([left, right], axis=1)
    choice = jnp.concatenate([choice, choice, choice], axis=0)
    parts = split3(fin_ref[...].reshape(members * points, cols))
    u_ref[...] = dot_nn(jnp.concatenate(parts, axis=1), choice)
    w = [params_ref[2 + k : 3 + k, :] for k in range(4)]
    acc = [jnp.zeros((8, slots), F32) for _ in range(members)]
    for i in range(points // 8):
        here = iota((8, slots), 0) + 8 * i
        at, under = here == spot, here == spot + 1
        a0 = jnp.where(at, w[0], 0.0) + jnp.where(under, w[2], 0.0)
        a1 = jnp.where(at, w[1], 0.0) + jnp.where(under, w[3], 0.0)
        for m in range(members):
            rows = slice(m * points + 8 * i, m * points + 8 * i + 8)
            acc[m] = acc[m] + a0 * u_ref[rows, 0:slots] + a1 * u_ref[rows, slots : 2 * slots]
    priors = [jnp.sum(v, axis=0, keepdims=True) for v in acc]
    halves = cols // LANES
    for g in range(nrows // 8):
        for h in range(halves):
            b = g * halves + h
            for m in range(members):
                for f in range(fields):
                    k = (m * fields + f) * 8
                    out_ref[b, k : k + 8, :] = fin_ref[
                        m, f * nrows + 8 * g : f * nrows + 8 * g + 8, h * LANES : (h + 1) * LANES
                    ]
                for q in range(slots // LANES):
                    k = members * fields * 8 + q * members + m
                    out_ref[b, k : k + 1, :] = priors[m][:, q * LANES : (q + 1) * LANES]


def load_priors(pri_ref, prior_ref):
    groups, held, _ = pri_ref.shape
    members = held * LANES // prior_ref.shape[1]
    for s in range(groups):
        for q in range(held // members):
            prior_ref[s * members : (s + 1) * members, q * LANES : (q + 1) * LANES] = pri_ref[
                s, q * members : (q + 1) * members, :
            ]


def partial_mixing(prior, value, error, loc):
    members = prior.shape[0]
    tiles = loc.shape[0]
    mean = jnp.sum(prior, axis=0, keepdims=True) * (1.0 / members)
    spread = prior - mean
    variance = jnp.sum(spread * spread, axis=0, keepdims=True) * (1.0 / (members - 1))
    error = jnp.where(error > 0.0, error, 1.0)
    total = variance + error
    root = jnp.sqrt(total)
    gain = (value - mean) / total - spread / (root * (jnp.sqrt(error) + root))
    gain = gain * (1.0 / (members - 1))
    groups = members // 8
    out = jnp.zeros((tiles * 8, LANES), F32)
    stacked = jnp.concatenate([spread] * groups, axis=0)
    group_of = iota(stacked.shape, 0) // members
    for k in range(groups):
        a = loc[:, None, :] * gain[None, 8 * k : 8 * k + 8, :]
        b = jnp.where(group_of == k, stacked, 0.0)
        out = out + dot_nt(a.reshape(tiles * 8, a.shape[2]), b, HI)
    return out.reshape(tiles, 8, LANES)


def unpack_mixing(packed_ref, members):
    packed = jnp.sum(packed_ref[...], axis=0)
    return jnp.concatenate(
        [packed[:, k * members : (k + 1) * members] for k in range(members // 8)], axis=0
    )


def first_kernel(pri_ref, params_ref, loc_ref, out_ref, prior_ref):
    load_priors(pri_ref, prior_ref)
    out_ref[...] = partial_mixing(
        prior_ref[:, 0:CAP], params_ref[6:7, 0:CAP], params_ref[7:8, 0:CAP], loc_ref[0]
    )


def second_kernel(w0_ref, pri_ref, params_ref, loc_ref, out_ref, prior_ref):
    load_priors(pri_ref, prior_ref)
    members = prior_ref.shape[0]
    w0 = unpack_mixing(w0_ref, members)
    prior = prior_ref[:, CAP : 2 * CAP]
    mean = jnp.sum(prior, axis=0, keepdims=True) * (1.0 / members)
    prior = prior + dot_nn(w0, prior - mean, HI)
    out_ref[...] = partial_mixing(
        prior, params_ref[6:7, CAP : 2 * CAP], params_ref[7:8, CAP : 2 * CAP], loc_ref[1]
    )


def apply_kernel(w0_ref, w1_ref, x_ref, out_ref):
    groups, held, _ = out_ref.shape
    own = 4
    members = groups * own
    fields = held // (own * 8)
    w0 = unpack_mixing(w0_ref, members)
    w1 = unpack_mixing(w1_ref, members)
    inv = 1.0 / members
    both = w0 + w1 + dot_nn(w1, w0 - jnp.sum(w0, axis=0, keepdims=True) * inv, HI)
    both = both - jnp.sum(both, axis=1, keepdims=True) * inv
    size = members * 8
    tall = jnp.where(iota((size, members), 0) // 8 == iota((size, members), 1), 1.0, 0.0)
    wide = jnp.where(iota((members, size), 1) // 8 == iota((members, size), 0), 1.0, 0.0)
    big = dot_nn(dot_nn(tall, both, HI), wide, HI)
    big = jnp.where(iota((size, size), 0) % 8 == iota((size, size), 1) % 8, big, 0.0)
    x = jnp.concatenate(
        [
            jnp.concatenate(
                [
                    x_ref[s, (m * fields + f) * 8 : (m * fields + f) * 8 + 8, :]
                    for s in range(groups)
                    for m in range(own)
                ],
                axis=0,
            )
            for f in range(fields)
        ],
        axis=1,
    )
    y = x + dot_nn(big, x, HI)
    for s in range(groups):
        for m in range(own):
            for f in range(fields):
                k = (m * fields + f) * 8
                n = (s * own + m) * 8
                out_ref[s, k : k + 8, :] = y[n : n + 8, f * LANES : (f + 1) * LANES]


def place_kernel(x_ref, out_ref):
    members, fields, nrows, cols = out_ref.shape
    halves = cols // LANES
    for g in range(nrows // 8):
        for h in range(halves):
            for m in range(members):
                for f in range(fields):
                    k = (m * fields + f) * 8
                    out_ref[m, f, 8 * g : 8 * g + 8, h * LANES : (h + 1) * LANES] = x_ref[
                        g * halves + h, k : k + 8, :
                    ]


VM = pltpu.VMEM
PARAMS = pltpu.CompilerParams(vmem_limit_bytes=32 << 20)


def shaped(shape, dtype=F32):
    return jax.ShapeDtypeStruct(shape, dtype)


def exchange(x, axis):
    return lax.all_to_all(x, axis, split_axis=0, concat_axis=0, tiled=False)


def on_device(x, smooth, cross, obs_tile, place, field, weights, values, error, loc):
    members, fields, nrows, cols = x.shape
    batches, count = place.shape
    tiles = lax.axis_size("dom")
    groups = lax.axis_size("mem")
    slots = batches * CAP
    mine = lax.axis_index("dom").astype(jnp.int32).reshape(1)
    smem = pl.BlockSpec(memory_space=pltpu.SMEM)
    vmem = pl.BlockSpec(memory_space=pltpu.VMEM)

    own_loc = loc[:, 0, :]
    all_loc = exchange(jnp.broadcast_to(own_loc[None], (tiles,) + own_loc.shape), "dom")

    tail = jnp.concatenate([x[:, :, nrows - 2 :], smooth[None, :, nrows - 2 :]], axis=0)
    head = jnp.concatenate([x[:, :, :2], smooth[None, :, :2]], axis=0)
    above = lax.ppermute(tail, "dom", [(i, i + 1) for i in range(tiles - 1)])
    below = lax.ppermute(head, "dom", [(i + 1, i) for i in range(tiles - 1)])

    rows = batches * count // LANES
    params, slot = pl.pallas_call(
        compact_kernel,
        out_shape=(shaped((8, slots)), shaped((rows, LANES), jnp.int32)),
        in_specs=[smem] + [vmem] * 6,
        scratch_shapes=[VM((rows, LANES), F32), VM((batches, 8, count), F32)],
        compiler_params=PARAMS,
        name="compact",
    )(mine, obs_tile.transpose(0, 2, 1), place, field, weights.transpose(0, 2, 1), values, error)

    own_rows = members * fields * 8
    prior_rows = members * slots // LANES
    blocks = nrows // 8 * (cols // LANES)
    points = fields * nrows
    sent = pl.pallas_call(
        forecast_kernel,
        out_shape=shaped((blocks, own_rows + prior_rows, LANES)),
        in_specs=[smem] + [vmem] * 5,
        scratch_shapes=[
            VM((members * fields, nrows + 32, cols), F32),
            VM((members * fields, nrows + 32, cols), F32),
            VM((fields, nrows + 32, cols), F32),
            VM((members, points, cols), F32),
            VM((members * points, 2 * slots), F32),
        ],
        compiler_params=PARAMS,
        name="forecast",
    )(cross, x, above, below, smooth, params)
    got = exchange(sent, "mem")

    loc_own = pl.pallas_call(
        localize_kernel,
        out_shape=shaped((batches, tiles, CAP)),
        compiler_params=PARAMS,
        name="localize",
    )(slot, all_loc.transpose(1, 0, 2))

    pri_spec = pl.BlockSpec((groups, prior_rows, LANES), lambda i: (0, own_rows // prior_rows, 0))
    state_spec = pl.BlockSpec((groups, own_rows, LANES), lambda i: (0, 0, 0))

    def whole(shape):
        return pl.BlockSpec(shape, lambda i: (0,) * len(shape))

    total = members * groups
    packed = (tiles, total * total // LANES, LANES)
    mix = dict(
        grid=(1,),
        out_shape=shaped(packed),
        out_specs=whole(packed),
        scratch_shapes=[VM((total, slots), F32)],
        compiler_params=PARAMS,
    )
    small = [pri_spec, whole(params.shape), whole(loc_own.shape)]
    w0 = pl.pallas_call(first_kernel, in_specs=small, name="first", **mix)(got, params, loc_own)
    w0 = exchange(w0, "dom")
    w1 = pl.pallas_call(second_kernel, in_specs=[whole(packed)] + small, name="second", **mix)(
        w0, got, params, loc_own
    )
    w1 = exchange(w1, "dom")
    back = pl.pallas_call(
        apply_kernel,
        grid=(1,),
        out_shape=shaped((groups, own_rows, LANES)),
        in_specs=[whole(packed), whole(packed), state_spec],
        out_specs=state_spec,
        compiler_params=PARAMS,
        name="apply",
    )(w0, w1, got)
    back = exchange(back, "mem")
    return pl.pallas_call(
        place_kernel, out_shape=shaped(x.shape), compiler_params=PARAMS, name="place"
    )(back)


def solution(mesh):
    placed = (
        P("mem", None, "dom", None),
        P(None, "dom", None),
        P(),
        P(),
        P(),
        P(),
        P(),
        P(),
        P(),
        P(None, "dom", None),
    )
    return jax.shard_map(
        on_device,
        mesh=mesh,
        in_specs=placed,
        out_specs=P("mem", None, "dom", None),
        check_vma=False,
    )
```

time: 405 us -> 83.4 us (0.21)
  blocking collectives: 208 us -> 37 us
  local copies, waits for them, and re-layouts: 113 us -> 1.85 us
  other arithmetic: 44.9 us -> 0.05 us
  waiting for transfers between devices: 0.9 us -> 15.6 us
  matrix products: 14.5 us -> 0 us
  between operations: 13.9 us -> 0.22 us
  Pallas kernels: 0 us -> 11 us
  starting transfers between devices: 9.47 us -> 17 us
    psum x2 -> x0, blocking collectives: 138 us -> none  [share_priors(): summed = lax.psum(masked, 'dom')]
    gather x2 -> x0, local copies, waits for them, and re-layouts: 70 us -> none  [local_priors(): jnp.take(flat, points, axis=1).reshape(sample_total_size, nobs_count, 4)]
    all_gather x2 -> x0, blocking collectives: 69.7 us -> none  [share_priors(): prior = lax.all_gather(summed, 'mem', axis=0, tiled=True)]
    all_to_all x0 -> x3, blocking collectives: none -> 37 us  [exchange(): return lax.all_to_all(x, axis, split_axis=0, concat_axis=0, tiled=False)]
    reduce_sum x10 -> x0, other arithmetic: 29.8 us -> none  [the longest x2 22.4 us: local_priors(): local_prior = jnp.sum(values * obs_weights[batch_index][None], axis=-1)]
    unnamed x33 -> x19, local copies, waits for them, and re-layouts: 19.3 us -> 0.84 us
    dot_general x6 -> x0, matrix products: 14.5 us -> none  [the longest x2 11.1 us: apply_update(): jnp.dot(own_columns.T, piece, precision=lax.Precision.HIGHEST, preferred_...]
    all_to_all x0 -> x2, waiting for transfers between devices: none -> 13.8 us  [exchange(): return lax.all_to_all(x, axis, split_axis=0, concat_axis=0, tiled=False)]
  transfers between devices with their start and end apart: 6 -> 4, of which waited for: 1 -> 2; matrix products, arithmetic and copies ran while one was open for 33% -> 0% of each run, Pallas kernels for 0% -> 8%
where the time goes in v1:
time: 83.4 us; the launch traced here: 82.7 us
  blocking collectives  37 us (44%)
  starting transfers between devices  17 us (20%)
  waiting for transfers between devices  15.6 us (19%)
  Pallas kernels  11 us (13%)
  local copies, waits for them, and re-layouts  1.85 us (2%)
    all_to_all x3, blocking collectives, exchange(): return lax.all_to_all(x, axis, split_axis=0, concat_axis=0, tiled=False)  37 us
    all_to_all x2, waiting for transfers between devices, exchange(): return lax.all_to_all(x, axis, split_axis=0, concat_axis=0, tiled=False)  13.8 us
    all_to_all x2, starting transfers between devices, exchange(): return lax.all_to_all(x, axis, split_axis=0, concat_axis=0, tiled=False)  13.3 us
    pallas_call x1, Pallas kernels, on_device(): pl.pallas_call(forecast_kernel, out_shape=shaped((blocks, own_rows + prio...  4.8 us
    ppermute x1, starting transfers between devices, on_device(): above = lax.ppermute(tail, 'dom', [(i, i + 1) for i in range(tiles - 1)])  2.44 us
    pallas_call x1, Pallas kernels, on_device(): pl.pallas_call(apply_kernel, grid=(1,), out_shape=shaped((groups, own_row...  1.99 us
    ppermute x1, waiting for transfers between devices, on_device(): below = lax.ppermute(head, 'dom', [(i + 1, i) for i in range(tiles - 1)])  1.78 us
  transfers between devices with their start and end apart: 4, of which 2 were waited for; matrix products, arithmetic and copies ran while one was open for 0% of the time, Pallas kernels for 8%

profile of v1, /device:TPU:0, one launch (start us, length us, event | category | flops | bytes accessed | tf_op | source)
XLA Modules:
  0.0 82.7 jit_solution(17561659830873519260)
XLA Ops:
  0.0 0.8 copy.16
  0.8 0.8 broadcast_in_dim.16
  1.6 6.6 %all-to-all-start.1 = ((f32[16,2,2048]{2,1,0:T(2,128)}), f32[16,2,2048]{2,1,0:T(2,128)S(1)}, u32[]{:S(2)}, u32[]{:S(2)}) async-start(f32[16,2,2048]{2,1,0:T(2,128)} %broadcast_in_dim.16), calls=%async_computation.1 | async-start | bytes 524288 | tf_op jit(solution)/shard_map/all_to_all | solution.py:295
  8.3 0.0 copy-start.6
  8.3 0.0 copy-start.7
  8.4 0.0 copy-start.2
  8.4 2.4 %collective-permute-start = (f32[5,5,2,256]{3,2,1,0:T(2,128)S(1)}, f32[5,5,2,256]{3,2,1,0:T(2,128)S(1)}, u32[]{:S(2)}, u32[]{:S(2)}) collective-permute-start(f32[5,5,2,256]{3,2,1,0:T(2,128)S(1)} %pad_maximum_fusion), channel_id=1, source_target_pairs={{0,1},{1,2},{2,3},{3,4},{4,5},{5,6},{6,7},{7,8},{8,9},{9,10},{10,1... | collective-permute-start | bytes 153608 | tf_op jit(solution)/shard_map/ppermute | solution.py:313
  10.9 0.0 copy-start.5
  10.9 1.3 %collective-permute-start.1 = (f32[5,5,2,256]{3,2,1,0:T(2,128)S(1)}, f32[5,5,2,256]{3,2,1,0:T(2,128)S(1)}, u32[]{:S(2)}, u32[]{:S(2)}) collective-permute-start(f32[5,5,2,256]{3,2,1,0:T(2,128)S(1)} %pad_maximum_fusion.1), channel_id=1, source_target_pairs={{1,0},{2,1},{3,2},{4,3},{5,4},{6,5},{7,6},{8,7},{9,8},{10,9},{11,1... | collective-permute-start | bytes 153608 | tf_op jit(solution)/shard_map/ppermute | solution.py:314
  12.3 1.1 %compact.1 = (f32[8,512]{1,0:T(8,128)S(1)}, s32[32,128]{1,0:T(8,128)S(1)}) custom-call(s32[1]{0:T(128)} %bitcast.2.tile_ref, s32[2,1,2048]{2,1,0:T(1,128)S(1)} %bitcast.15, s32[2,2048]{1,0:T(2,128)S(1)} %copy-done.4, s32[2,2048]{1,0:T(2,128)S(1)} %copy-done.5, f32[2,4,2048]{2,1,0:T(4,128)S(1)} %bitcast.14, f32[2,2048]{1,0:T(2,128)S(1)} %copy-done.6, ...), custom_call_target="tpu_custom_call" | custom-call | tf_op jit(solution)/shard_map/compact/pallas_call | solution.py:317
  13.4 0.0 collective-permute-done.above_ref
  13.4 1.8 %collective-permute-done.1.below_ref = f32[5,5,2,256]{3,2,1,0:T(2,128)S(1)} collective-permute-done((f32[5,5,2,256]{3,2,1,0:T(2,128)S(1)}, f32[5,5,2,256]{3,2,1,0:T(2,128)S(1)}, u32[]{:S(2)}, u32[]{:S(2)}) %collective-permute-start.1) | collective-permute-done | bytes 51232 | tf_op jit(solution)/shard_map/ppermute | solution.py:314
  15.2 4.8 %forecast.1 = f32[8,176,128]{2,1,0:T(8,128)} custom-call(f32[5,5]{1,0:T(8,128)S(1)} %copy-done.8, f32[4,5,32,256]{3,2,1,0:T(8,128)S(1)} %copy-done, f32[5,5,2,256]{3,2,1,0:T(2,128)S(1)} %collective-permute-done.above_ref, f32[5,5,2,256]{3,2,1,0:T(2,128)S(1)} %collective-permute-done.1.below_ref, f32[5,32,256]{2,1,0:T(8,128)S(1)} %copy-done.1, ...), custom_call_target="tpu_custom_call" | custom-call | tf_op jit(solution)/shard_map/forecast/pallas_call | solution.py:330
  20.0 6.6 %all-to-all-start = ((f32[8,176,128]{2,1,0:T(8,128)}), f32[8,176,128]{2,1,0:T(8,128)S(1)}, u32[]{:S(2)}, u32[]{:S(2)}) async-start(f32[8,176,128]{2,1,0:T(8,128)} %forecast.1), calls=%async_computation | async-start | bytes 1441792 | tf_op jit(solution)/shard_map/all_to_all | solution.py:295
  26.6 0.2 copy.15
  26.8 0.7 localize.1.loc_ref
  27.5 13.8 %all-to-all-done.pri_ref.x_ref = f32[8,176,128]{2,1,0:T(8,128)S(1)} async-done(((f32[8,176,128]{2,1,0:T(8,128)}), f32[8,176,128]{2,1,0:T(8,128)S(1)}, u32[]{:S(2)}, u32[]{:S(2)}) %all-to-all-start) | async-done | bytes 720928 | tf_op jit(solution)/shard_map/all_to_all | solution.py:295
  41.3 0.6 first.1
  41.9 12.3 %all_to_all.25.w0_ref = f32[16,8,128]{2,1,0:T(8,128)S(1)} all-to-all(f32[16,8,128]{2,1,0:T(8,128)S(1)} %first.1), channel_id=1, replica_groups=mesh['mem'=8,'dom'=16] {'dom'}, dimensions={0} | all-to-all | bytes 131072 | tf_op jit(solution)/shard_map/all_to_all | solution.py:295
  54.3 0.9 %second.1 = f32[16,8,128]{2,1,0:T(8,128)S(1)} custom-call(f32[16,8,128]{2,1,0:T(8,128)S(1)} %all_to_all.25.w0_ref, f32[8,176,128]{2,1,0:T(8,128)S(1)} %all-to-all-done.pri_ref.x_ref, f32[8,512]{1,0:T(8,128)S(1)} %get-tuple-element.7.params_ref, f32[2,16,256]{2,1,0:T(8,128)S(1)} %localize.1.loc_ref), custom_call_target="tpu_custom_call" | custom-call | tf_op jit(solution)/shard_map/second/pallas_call | solution.py:371
  55.1 8.7 %all_to_all.26.w1_ref = f32[16,8,128]{2,1,0:T(8,128)S(1)} all-to-all(f32[16,8,128]{2,1,0:T(8,128)S(1)} %second.1), channel_id=1, replica_groups=mesh['mem'=8,'dom'=16] {'dom'}, dimensions={0} | all-to-all | bytes 131072 | tf_op jit(solution)/shard_map/all_to_all | solution.py:295
  63.8 2.0 %apply.1 = f32[8,160,128]{2,1,0:T(8,128)S(1)} custom-call(f32[16,8,128]{2,1,0:T(8,128)S(1)} %all_to_all.25.w0_ref, f32[16,8,128]{2,1,0:T(8,128)S(1)} %all_to_all.26.w1_ref, f32[8,176,128]{2,1,0:T(8,128)S(1)} %all-to-all-done.pri_ref.x_ref), custom_call_target="tpu_custom_call" | custom-call | tf_op jit(solution)/shard_map/apply/pallas_call | solution.py:375
  65.8 15.9 %all_to_all.27.x_ref = f32[8,160,128]{2,1,0:T(8,128)S(1)} all-to-all(f32[8,160,128]{2,1,0:T(8,128)S(1)} %apply.1), channel_id=1, replica_groups=mesh['mem'=8,'dom'=16] {'mem'}, dimensions={0} | all-to-all | bytes 1310720 | tf_op jit(solution)/shard_map/all_to_all | solution.py:295
  81.7 0.9 %place.1 = f32[4,5,32,256]{3,2,1,0:T(8,128)} custom-call(f32[8,160,128]{2,1,0:T(8,128)S(1)} %all_to_all.27.x_ref), custom_call_target="tpu_custom_call" | custom-call | tf_op jit(solution)/shard_map/place/pallas_call | solution.py:385
  (19 shorter events, 0.1 us)
Async XLA Ops:
  0.0 8.3 %copy-start = (f32[4,5,32,256]{3,2,1,0:T(8,128)S(1)}, f32[4,5,32,256]{3,2,1,0:T(8,128)}, u32[]{:S(2)}) copy-start(f32[4,5,32,256]{3,2,1,0:T(8,128)} %x_ref.1) | copy-start | bytes 1966084
  1.6 6.7 %copy-start.1 = (f32[5,32,256]{2,1,0:T(8,128)S(1)}, f32[5,32,256]{2,1,0:T(8,128)}, u32[]{:S(2)}) copy-start(f32[5,32,256]{2,1,0:T(8,128)} %smooth_ref.1) | copy-start | bytes 491524
  1.6 18.4 %all-to-all-start.1 = ((f32[16,2,2048]{2,1,0:T(2,128)}), f32[16,2,2048]{2,1,0:T(2,128)S(1)}, u32[]{:S(2)}, u32[]{:S(2)}) async-start(f32[16,2,2048]{2,1,0:T(2,128)} %broadcast_in_dim.16), calls=%async_computation.1 | async-start | bytes 524288 | tf_op jit(solution)/shard_map/all_to_all | solution.py:295
  8.3 3.9 %copy-start.6 = (f32[2,2048]{1,0:T(2,128)S(1)}, f32[2,2048]{1,0:T(2,128)}, u32[]{:S(2)}) copy-start(f32[2,2048]{1,0:T(2,128)} %value_ref.1) | copy-start | bytes 49156
  8.3 3.9 %copy-start.7 = (f32[2,2048]{1,0:T(2,128)S(1)}, f32[2,2048]{1,0:T(2,128)}, u32[]{:S(2)}) copy-start(f32[2,2048]{1,0:T(2,128)} %error_ref.1) | copy-start | bytes 49156
  8.4 3.9 %copy-start.2 = (f32[2,2048,4]{1,2,0:T(4,128)S(1)}, f32[2,2048,4]{1,2,0:T(4,128)}, u32[]{:S(2)}) copy-start(f32[2,2048,4]{1,2,0:T(4,128)} %param.16) | copy-start | bytes 196612
  8.4 5.0 %collective-permute-start = (f32[5,5,2,256]{3,2,1,0:T(2,128)S(1)}, f32[5,5,2,256]{3,2,1,0:T(2,128)S(1)}, u32[]{:S(2)}, u32[]{:S(2)}) collective-permute-start(f32[5,5,2,256]{3,2,1,0:T(2,128)S(1)} %pad_maximum_fusion), channel_id=1, source_target_pairs={{0,1},{1,2},{2,3},{3,4},{4,5},{5,6},{6,7},{7,8},{8,9},{9,10},{10,1... | collective-permute-start | bytes 153608 | tf_op jit(solution)/shard_map/ppermute | solution.py:313
  10.9 1.4 %copy-start.3 = (s32[2,2048,1]{1,2,0:T(1,128)S(1)}, s32[2,2048,1]{1,2,0:T(1,128)}, u32[]{:S(2)}) copy-start(s32[2,2048,1]{1,2,0:T(1,128)} %param.13) | copy-start | bytes 49156
  10.9 1.4 %copy-start.4 = (s32[2,2048]{1,0:T(2,128)S(1)}, s32[2,2048]{1,0:T(2,128)}, u32[]{:S(2)}) copy-start(s32[2,2048]{1,0:T(2,128)} %place_ref.1) | copy-start | bytes 49156
  10.9 1.4 %copy-start.5 = (s32[2,2048]{1,0:T(2,128)S(1)}, s32[2,2048]{1,0:T(2,128)}, u32[]{:S(2)}) copy-start(s32[2,2048]{1,0:T(2,128)} %field_ref.1) | copy-start | bytes 49156
  10.9 4.3 %collective-permute-start.1 = (f32[5,5,2,256]{3,2,1,0:T(2,128)S(1)}, f32[5,5,2,256]{3,2,1,0:T(2,128)S(1)}, u32[]{:S(2)}, u32[]{:S(2)}) collective-permute-start(f32[5,5,2,256]{3,2,1,0:T(2,128)S(1)} %pad_maximum_fusion.1), channel_id=1, source_target_pairs={{1,0},{2,1},{3,2},{4,3},{5,4},{6,5},{7,6},{8,7},{9,8},{10,9},{11,1... | collective-permute-start | bytes 153608 | tf_op jit(solution)/shard_map/ppermute | solution.py:314
  12.3 2.9 %copy-start.8 = (f32[5,5]{1,0:T(8,128)S(1)}, f32[5,5]{1,0:T(8,128)}, u32[]{:S(2)}) copy-start(f32[5,5]{1,0:T(8,128)} %cross_ref.1) | copy-start | bytes 304
  20.0 21.3 %all-to-all-start = ((f32[8,176,128]{2,1,0:T(8,128)}), f32[8,176,128]{2,1,0:T(8,128)S(1)}, u32[]{:S(2)}, u32[]{:S(2)}) async-start(f32[8,176,128]{2,1,0:T(8,128)} %forecast.1), calls=%async_computation | async-start | bytes 1441792 | tf_op jit(solution)/shard_map/all_to_all | solution.py:295

commit v2 on v1

v2 whole, which is shorter than its diff:
```python
import jax
import jax.numpy as jnp
from jax import lax
from jax.experimental import pallas as pl
from jax.experimental.pallas import tpu as pltpu
from jax.sharding import PartitionSpec as P

F32 = jnp.float32
BF16 = jnp.bfloat16
HI = lax.Precision.HIGHEST
CAP = 256
LANES = 128
STEPS = (2, 4, 8, 1)


def split3(values):
    high = values.astype(BF16)
    rest = values - high.astype(F32)
    middle = rest.astype(BF16)
    low = (rest - middle.astype(F32)).astype(BF16)
    return high, middle, low


def dot_nt(a, b, precision=None):
    return lax.dot_general(
        a, b, (((1,), (1,)), ((), ())), precision=precision, preferred_element_type=F32
    )


def dot_nn(a, b, precision=None):
    return lax.dot_general(
        a, b, (((1,), (0,)), ((), ())), precision=precision, preferred_element_type=F32
    )


def iota(shape, dim):
    return lax.broadcasted_iota(jnp.int32, shape, dim)


def chosen_rows(slots, row):
    return jnp.where(slots[row : row + 1, :] == iota((CAP, LANES), 0), 1.0, 0.0).astype(BF16)


def substep(src_ref, cross_ref, smooth, m, base):
    fields = len(smooth)
    cols = src_ref.shape[2]
    lane = iota((8, cols), 1)
    own = [src_ref[m * fields + f, base : base + 8, :] for f in range(fields)]
    result = []
    for f in range(fields):
        v = own[f]
        lap = src_ref[m * fields + f, base + 1 : base + 9, :]
        lap = lap + src_ref[m * fields + f, base - 1 : base + 7, :]
        lap = lap + jnp.where(lane == cols - 1, 0.0, pltpu.roll(v, cols - 1, 1))
        lap = lap + jnp.where(lane == 0, 0.0, pltpu.roll(v, 1, 1)) - 4.0 * v
        mixed = cross_ref[f, 0] * own[0]
        for g in range(1, fields):
            mixed = mixed + cross_ref[f, g] * own[g]
        result.append(v + smooth[f] * lap + mixed)
    return result


def interior_kernel(tile_ref, cross_ref, x_ref, smooth_ref, owner_ref, place_ref, field_ref,
                    weight_ref, value_ref, error_ref,
                    params_ref, slots_ref, inner_ref, strip_ref, smooth_strip_ref,
                    mask_ref, vals_ref, buf_ref, nxt_ref, sem):
    planes, nrows, cols = x_ref.shape
    members, points, _ = inner_ref.shape
    fields = points // nrows
    last = TOP + nrows
    load = pltpu.make_async_copy(x_ref, buf_ref.at[:, pl.ds(TOP, nrows), :], sem)
    load.start()
    compact(tile_ref, owner_ref, place_ref, field_ref, weight_ref, value_ref, error_ref,
            params_ref, slots_ref, mask_ref, vals_ref)
    for f in range(fields):
        smooth_strip_ref[f, 3:8, :] = smooth_ref[f, 0:5, :]
        smooth_strip_ref[f, 8:13, :] = smooth_ref[f, nrows - 5 : nrows, :]
    load.wait()
    for p in range(planes):
        strip_ref[p, 3:8, :] = buf_ref[p, TOP : TOP + 5, :]
        strip_ref[p, 8:13, :] = buf_ref[p, last - 5 : last, :]

    def member(m, carry):
        for g in range(nrows // 8):
            smooth = [smooth_ref[f, 8 * g : 8 * g + 8, :] for f in range(fields)]
            for f, v in enumerate(substep(buf_ref, cross_ref, smooth, m, TOP + 8 * g)):
                nxt_ref[m * fields + f, TOP + 8 * g : TOP + 8 * g + 8, :] = v
        for g in range(nrows // 8):
            smooth = [smooth_ref[f, 8 * g : 8 * g + 8, :] for f in range(fields)]
            for f, v in enumerate(substep(nxt_ref, cross_ref, smooth, m, TOP + 8 * g)):
                inner_ref[m, f * nrows + 8 * g : f * nrows + 8 * g + 8, :] = v
        return carry

    lax.fori_loop(0, members, member, 0)


def compact(tile_ref, owner_ref, place_ref, field_ref, weight_ref, value_ref, error_ref,
            params_ref, slots_ref, mask_ref, vals_ref):
    batches, _, count = owner_ref.shape
    chunks = count // LANES
    rows = batches * chunks
    mine = tile_ref[0]
    for b in range(batches):
        own = jnp.where(owner_ref[b] == mine, 1.0, 0.0)
        for j in range(chunks):
            mask_ref[b * chunks + j : b * chunks + j + 1, :] = own[:, j * LANES : (j + 1) * LANES]
    mask = mask_ref[...]
    mask16 = mask.astype(BF16)
    upper = jnp.where(iota((LANES, LANES), 0) <= iota((LANES, LANES), 1), 1.0, 0.0).astype(BF16)
    inside = dot_nn(mask16, upper)
    totals = dot_nn(mask16, jnp.ones((LANES, LANES), BF16)).astype(BF16)
    a, c = iota((rows, rows), 0), iota((rows, rows), 1)
    before = jnp.where((c < a) & ((c >= chunks) == (a >= chunks)), 1.0, 0.0).astype(BF16)
    rank = inside + dot_nn(before, totals) - 1.0
    slots = jnp.where(mask > 0.5, rank, -1.0).astype(jnp.int32)
    slots_ref[...] = slots
    for b in range(batches):
        place = place_ref[b : b + 1, :]
        row = ((place.astype(F32) + 0.5) * (1.0 / 255.0)).astype(jnp.int32)
        vals_ref[b, 0:1, :] = (field_ref[b : b + 1, :] * 32 + row).astype(F32)
        vals_ref[b, 1:2, :] = (place - row * 255).astype(F32)
        vals_ref[b, 2:6, :] = weight_ref[b]
        vals_ref[b, 6:7, :] = value_ref[b : b + 1, :]
        vals_ref[b, 7:8, :] = error_ref[b : b + 1, :]
        total = jnp.zeros((24, CAP), F32)
        for j in range(chunks):
            parts = split3(vals_ref[b, :, j * LANES : (j + 1) * LANES])
            total = total + dot_nt(
                jnp.concatenate([p.astype(F32) for p in parts], axis=0).astype(BF16),
                chosen_rows(slots, b * chunks + j),
            )
        params_ref[:, b * CAP : (b + 1) * CAP] = total[0:8] + total[8:16] + total[16:24]


def localize_kernel(slots_ref, near_ref, far_ref, out_ref):
    batches, tiles, _ = out_ref.shape
    slots = slots_ref[...]
    rows = slots.shape[0]
    chunks = rows // batches
    for b in range(batches):
        total = jnp.zeros((3 * tiles, CAP), F32)
        for j in range(chunks):
            at = pl.ds(b * chunks + j, tiles // 2, stride=rows)
            parts = split3(jnp.concatenate([near_ref[at, :], far_ref[at, :]], axis=0))
            total = total + dot_nt(
                jnp.concatenate(parts, axis=0), chosen_rows(slots, b * chunks + j)
            )
        out_ref[b] = total[:tiles] + total[tiles : 2 * tiles] + total[2 * tiles :]


TOP = 16


def forecast_kernel(cross_ref, inner_ref, strip_ref, smooth_strip_ref, above_ref, below_ref,
                    params_ref, out_ref, buf_ref, nxt_ref, sm_ref, fin_ref, u_ref, state_ref,
                    prior_ref, sems):
    members, points, cols = inner_ref.shape
    _, fields, _, _ = above_ref.shape
    nrows = points // fields
    fin_ref[...] = inner_ref[...]
    sm_ref[...] = smooth_strip_ref[...]
    for f in range(fields):
        sm_ref[f, 2:3, :] = above_ref[members, f, 1:2, :]
        sm_ref[f, 13:14, :] = below_ref[members, f, 0:1, :]
    for m in range(members):
        for f in range(fields):
            p = m * fields + f
            buf_ref[p, 8:24, :] = strip_ref[p]
            buf_ref[p, 9:11, :] = above_ref[m, f]
            buf_ref[p, 21:23, :] = below_ref[m, f]

    def member(m, carry):
        for h in range(2):
            smooth = [sm_ref[f, 8 * h : 8 * h + 8, :] for f in range(fields)]
            for f, v in enumerate(substep(buf_ref, cross_ref, smooth, m, 8 + 8 * h)):
                nxt_ref[m * fields + f, 8 + 8 * h : 16 + 8 * h, :] = v
        for h in range(2):
            smooth = [sm_ref[f, 8 * h : 8 * h + 8, :] for f in range(fields)]
            for f, v in enumerate(substep(nxt_ref, cross_ref, smooth, m, 8 + 8 * h)):
                at = f * nrows + h * (nrows - 2)
                fin_ref[m, at : at + 2, :] = v[3:5]
        return carry

    lax.fori_loop(0, members, member, 0)

    halves = cols // LANES
    own_rows = members * fields * 8
    for g in range(nrows // 8):
        for h in range(halves):
            for m in range(members):
                for f in range(fields):
                    k = (m * fields + f) * 8
                    state_ref[g * halves + h, k : k + 8, :] = fin_ref[
                        m, f * nrows + 8 * g : f * nrows + 8 * g + 8, h * LANES : (h + 1) * LANES
                    ]
    send = pltpu.make_async_copy(state_ref, out_ref.at[:, pl.ds(0, own_rows), :], sems.at[0])
    send.start()

    slots = params_ref.shape[1]
    spot = params_ref[0:1, :].astype(jnp.int32)
    column = params_ref[1:2, :].astype(jnp.int32)
    cid = iota((cols, slots), 0)
    left = jnp.where(cid == column, 1.0, 0.0).astype(BF16)
    right = jnp.where(cid == column + 1, 1.0, 0.0).astype(BF16)
    choice = jnp.concatenate([left, right], axis=1)
    choice = jnp.concatenate([choice, choice], axis=0)
    parts = split3(fin_ref[...].reshape(members * points, cols))[:2]
    u_ref[...] = dot_nn(jnp.concatenate(parts, axis=1), choice)
    w = [params_ref[2 + k : 3 + k, :] for k in range(4)]
    acc = [jnp.zeros((8, slots), F32) for _ in range(members)]
    for i in range(points // 8):
        here = iota((8, slots), 0) + 8 * i
        at, under = here == spot, here == spot + 1
        a0 = jnp.where(at, w[0], 0.0) + jnp.where(under, w[2], 0.0)
        a1 = jnp.where(at, w[1], 0.0) + jnp.where(under, w[3], 0.0)
        for m in range(members):
            rows = slice(m * points + 8 * i, m * points + 8 * i + 8)
            acc[m] = acc[m] + a0 * u_ref[rows, 0:slots] + a1 * u_ref[rows, slots : 2 * slots]
    for m in range(members):
        row = jnp.sum(acc[m], axis=0, keepdims=True)
        for q in range(slots // LANES):
            piece = row[:, q * LANES : (q + 1) * LANES]
            for b in range(nrows // 8 * halves):
                prior_ref[b, q * members + m : q * members + m + 1, :] = piece
    held = slots // LANES * members
    send_priors = pltpu.make_async_copy(
        prior_ref, out_ref.at[:, pl.ds(own_rows, held), :], sems.at[1]
    )
    send_priors.start()
    send.wait()
    send_priors.wait()


def load_priors(got_ref, prior_ref):
    groups, rows, _ = got_ref.shape
    total, slots = prior_ref.shape
    members = total // groups
    pieces = slots // LANES
    first = rows - pieces * members
    for s in range(groups):
        for q in range(pieces):
            k = first + q * members
            prior_ref[s * members : (s + 1) * members, q * LANES : (q + 1) * LANES] = got_ref[
                s, k : k + members, :
            ]


def distance(k):
    return sum(step for i, step in enumerate(STEPS) if (k >> i) & 1)


def partial_mixing(tile_ref, out_ref, prior, value, error, loc):
    members = prior.shape[0]
    tiles = loc.shape[0]
    mean = jnp.sum(prior, axis=0, keepdims=True) * (1.0 / members)
    spread = prior - mean
    variance = jnp.sum(spread * spread, axis=0, keepdims=True) * (1.0 / (members - 1))
    error = jnp.where(error > 0.0, error, 1.0)
    total = variance + error
    root = jnp.sqrt(total)
    gain = (value - mean) / total - spread / (root * (jnp.sqrt(error) + root))
    gain = gain * (1.0 / (members - 1))
    groups = members // 8
    out = jnp.zeros((tiles * 8, LANES), F32)
    stacked = jnp.concatenate([spread] * groups, axis=0)
    group_of = iota(stacked.shape, 0) // members
    for k in range(groups):
        a = loc[:, None, :] * gain[None, 8 * k : 8 * k + 8, :]
        b = jnp.where(group_of == k, stacked, 0.0)
        out = out + dot_nt(a.reshape(tiles * 8, a.shape[2]), b, HI)
    mine = tile_ref[0]
    for k in range(tiles):
        out_ref[mine ^ distance(k)] = out[8 * k : 8 * k + 8]


def unpack_mixing(packed_ref, members):
    packed = jnp.sum(packed_ref[...], axis=0)
    return jnp.concatenate(
        [packed[:, k * members : (k + 1) * members] for k in range(members // 8)], axis=0
    )


def first_kernel(tile_ref, pri_ref, params_ref, loc_ref, out_ref, prior_ref):
    load_priors(pri_ref, prior_ref)
    value, error = params_ref[6:7, 0:CAP], params_ref[7:8, 0:CAP]
    partial_mixing(tile_ref, out_ref, prior_ref[:, 0:CAP], value, error, loc_ref[0])


def second_kernel(tile_ref, w0_ref, pri_ref, params_ref, loc_ref, out_ref, prior_ref):
    load_priors(pri_ref, prior_ref)
    members = prior_ref.shape[0]
    w0 = unpack_mixing(w0_ref, members)
    prior = prior_ref[:, CAP : 2 * CAP]
    mean = jnp.sum(prior, axis=0, keepdims=True) * (1.0 / members)
    prior = prior + dot_nn(w0, prior - mean, HI)
    value, error = params_ref[6:7, CAP : 2 * CAP], params_ref[7:8, CAP : 2 * CAP]
    partial_mixing(tile_ref, out_ref, prior, value, error, loc_ref[1])


def apply_kernel(w0_ref, w1_ref, x_ref, out_ref):
    groups, held, _ = out_ref.shape
    own = 4
    members = groups * own
    fields = held // (own * 8)
    w0 = unpack_mixing(w0_ref, members)
    w1 = unpack_mixing(w1_ref, members)
    inv = 1.0 / members
    both = w0 + w1 + dot_nn(w1, w0 - jnp.sum(w0, axis=0, keepdims=True) * inv, HI)
    both = both - jnp.sum(both, axis=1, keepdims=True) * inv
    size = members * 8
    tall = jnp.where(iota((size, members), 0) // 8 == iota((size, members), 1), 1.0, 0.0)
    wide = jnp.where(iota((members, size), 1) // 8 == iota((members, size), 0), 1.0, 0.0)
    big = dot_nn(dot_nn(tall, both, HI), wide, HI)
    big = jnp.where(iota((size, size), 0) % 8 == iota((size, size), 1) % 8, big, 0.0)
    x = jnp.concatenate(
        [
            jnp.concatenate(
                [
                    x_ref[s, (m * fields + f) * 8 : (m * fields + f) * 8 + 8, :]
                    for s in range(groups)
                    for m in range(own)
                ],
                axis=0,
            )
            for f in range(fields)
        ],
        axis=1,
    )
    big_high, big_low, _ = split3(big)
    x_high, x_low, _ = split3(x)
    y = dot_nn(
        jnp.concatenate([big_high, big_low, big_high], axis=1),
        jnp.concatenate([x_high, x_high, x_low], axis=0),
    )
    y = x + y
    for s in range(groups):
        for m in range(own):
            for f in range(fields):
                k = (m * fields + f) * 8
                n = (s * own + m) * 8
                out_ref[s, k : k + 8, :] = y[n : n + 8, f * LANES : (f + 1) * LANES]


def place_kernel(x_ref, out_ref, sems):
    _, nrows, cols = out_ref.shape
    halves = cols // LANES
    copies = []
    for b in range(nrows // 8 * halves):
        g, h = b // halves, b % halves
        to = out_ref.at[:, pl.ds(8 * g, 8), pl.ds(h * LANES, LANES)]
        copies.append(pltpu.make_async_copy(x_ref.at[b], to, sems.at[b]))
        copies[-1].start()
    for copy in copies:
        copy.wait()


VM = pltpu.VMEM
PARAMS = pltpu.CompilerParams(vmem_limit_bytes=32 << 20)


def shaped(shape, dtype=F32):
    return jax.ShapeDtypeStruct(shape, dtype)


def swap(x, distance):
    count = lax.axis_size("dom")
    return lax.ppermute(x, "dom", [(i, i ^ distance) for i in range(count)])


def exchange(x, axis):
    return lax.all_to_all(x, axis, split_axis=0, concat_axis=0, tiled=False)


def on_device(x, smooth, cross, obs_tile, place, field, weights, values, error, loc):
    members, fields, nrows, cols = x.shape
    batches, count = place.shape
    tiles = lax.axis_size("dom")
    groups = lax.axis_size("mem")
    slots = batches * CAP
    mine = lax.axis_index("dom").astype(jnp.int32).reshape(1)
    smem = pl.BlockSpec(memory_space=pltpu.SMEM)
    vmem = pl.BlockSpec(memory_space=pltpu.VMEM)

    rows = batches * count // LANES
    held = loc.reshape(rows, LANES)
    held = jnp.concatenate([held, swap(held, STEPS[0])], axis=0)

    tail = jnp.concatenate([x[:, :, nrows - 2 :], smooth[None, :, nrows - 2 :]], axis=0)
    head = jnp.concatenate([x[:, :, :2], smooth[None, :, :2]], axis=0)
    above = lax.ppermute(tail, "dom", [(i, i + 1) for i in range(tiles - 1)])
    below = lax.ppermute(head, "dom", [(i + 1, i) for i in range(tiles - 1)])

    points = fields * nrows
    planes = members * fields
    hbm = pl.BlockSpec(memory_space=pltpu.HBM)
    params, slot, inner, strip, smooth_strip = pl.pallas_call(
        interior_kernel,
        out_shape=(
            shaped((8, slots)),
            shaped((rows, LANES), jnp.int32),
            shaped((members, points, cols)),
            shaped((planes, 16, cols)),
            shaped((fields, 16, cols)),
        ),
        in_specs=[smem, smem, hbm] + [vmem] * 7,
        scratch_shapes=[
            VM((rows, LANES), F32),
            VM((batches, 8, count), F32),
            VM((planes, nrows + 32, cols), F32),
            VM((planes, nrows + 32, cols), F32),
            pltpu.SemaphoreType.DMA,
        ],
        compiler_params=PARAMS,
        name="interior",
    )(
        mine, cross, pltpu.with_memory_space_constraint(x.reshape(planes, nrows, cols), pltpu.HBM), smooth, obs_tile.transpose(0, 2, 1), place,
        field, weights.transpose(0, 2, 1), values, error,
    )

    held, above, below, params = lax.optimization_barrier((held, above, below, params))
    held = jnp.concatenate([held, swap(held, STEPS[1])], axis=0)

    own_rows = members * fields * 8
    prior_rows = members * slots // LANES
    blocks = nrows // 8 * (cols // LANES)
    sent = pl.pallas_call(
        forecast_kernel,
        out_shape=shaped((blocks, own_rows + prior_rows, LANES)),
        in_specs=[smem] + [vmem] * 6,
        out_specs=hbm,
        scratch_shapes=[
            VM((planes, 32, cols), F32),
            VM((planes, 32, cols), F32),
            VM((fields, 16, cols), F32),
            VM((members, points, cols), F32),
            VM((members * points, 2 * slots), F32),
            VM((blocks, own_rows, LANES), F32),
            VM((blocks, prior_rows, LANES), F32),
            pltpu.SemaphoreType.DMA((2,)),
        ],
        compiler_params=PARAMS,
        name="forecast",
    )(cross, inner, strip, smooth_strip, above, below, params)
    held, sent = lax.optimization_barrier((held, sent))
    got = exchange(sent, "mem")
    held = jnp.concatenate([held, swap(held, STEPS[2])], axis=0)

    loc_own = pl.pallas_call(
        localize_kernel,
        out_shape=shaped((batches, tiles, CAP)),
        compiler_params=PARAMS,
        name="localize",
    )(slot, held, swap(held, STEPS[3]))

    total = members * groups
    mix = dict(
        out_shape=shaped((tiles, total * total // LANES, LANES)),
        scratch_shapes=[VM((total, slots), F32)],
        compiler_params=PARAMS,
    )
    w0 = pl.pallas_call(first_kernel, in_specs=[smem] + [vmem] * 3, name="first", **mix)(
        mine, got, params, loc_own
    )
    w0 = exchange(w0, "dom")
    w1 = pl.pallas_call(second_kernel, in_specs=[smem] + [vmem] * 4, name="second", **mix)(
        mine, w0, got, params, loc_own
    )
    w1 = exchange(w1, "dom")
    back = pl.pallas_call(
        apply_kernel,
        out_shape=shaped((groups, own_rows, LANES)),
        compiler_params=PARAMS,
        name="apply",
    )(w0, w1, got)
    back = exchange(back, "mem")
    back = pl.pallas_call(
        place_kernel,
        out_shape=shaped((planes, nrows, cols)),
        out_specs=hbm,
        scratch_shapes=[pltpu.SemaphoreType.DMA((blocks,))],
        compiler_params=PARAMS,
        name="place",
    )(back.reshape(blocks, planes, 8, LANES))
    return back.reshape(x.shape)


def solution(mesh):
    placed = (
        P("mem", None, "dom", None),
        P(None, "dom", None),
        P(),
        P(),
        P(),
        P(),
        P(),
        P(),
        P(),
        P(None, "dom", None),
    )
    return jax.shard_map(
        on_device,
        mesh=mesh,
        in_specs=placed,
        out_specs=P("mem", None, "dom", None),
        check_vma=False,
    )
```

time: 83.4 us -> 79.6 us (0.954)
  waiting for transfers between devices: 15.6 us -> 7.48 us
  starting transfers between devices: 17 us -> 20.5 us
    ppermute x0 -> x4, starting transfers between devices: none -> 10.9 us  [swap(): return lax.ppermute(x, 'dom', [(i, i ^ distance) for i in range(count)])]
    all_to_all x2 -> x1, waiting for transfers between devices: 13.8 us -> 3.9 us  [exchange(): return lax.all_to_all(x, axis, split_axis=0, concat_axis=0, tiled=False)]
    all_to_all x2 -> x1, starting transfers between devices: 13.3 us -> 6.65 us  [exchange(): return lax.all_to_all(x, axis, split_axis=0, concat_axis=0, tiled=False)]
    ppermute x0 -> x4, waiting for transfers between devices: none -> 3.58 us  [swap(): return lax.ppermute(x, 'dom', [(i, i ^ distance) for i in range(count)])]
    pallas_call x5, Pallas kernels: 5.47 us -> 7.28 us  [the longest x1 3.25 us: on_device(): pl.pallas_call(interior_kernel, out_shape=(shaped((8, slots)), shaped((ro...]
    ppermute x1, waiting for transfers between devices: 1.78 us -> 0.01 us  [on_device(): below = lax.ppermute(head, 'dom', [(i + 1, i) for i in range(tiles - 1)])]
    pallas_call x1, Pallas kernels: 4.8 us -> 3.62 us  [on_device(): pl.pallas_call(forecast_kernel, out_shape=shaped((blocks, own_rows + prio...]
    slice x1, local copies, waits for them, and re-layouts: 0.03 us -> 1.07 us  [on_device(): head = jnp.concatenate([x[:, :, :2], smooth[None, :, :2]], axis=0)]
  transfers between devices with their start and end apart: 4 -> 7, of which waited for: 2 -> 3; matrix products, arithmetic and copies ran while one was open for 0% -> 2% of each run, Pallas kernels for 8% -> 10%
where the time goes in v2:
time: 79.6 us; the launch traced here: 78.9 us
  blocking collectives  36.4 us (46%)
  starting transfers between devices  20.5 us (26%)
  Pallas kernels  11.6 us (15%)
  waiting for transfers between devices  7.48 us (9%)
  local copies, waits for them, and re-layouts  2.54 us (3%)
    all_to_all x3, blocking collectives, exchange(): return lax.all_to_all(x, axis, split_axis=0, concat_axis=0, tiled=False)  36.4 us
    ppermute x4, starting transfers between devices, swap(): return lax.ppermute(x, 'dom', [(i, i ^ distance) for i in range(count)])  10.9 us
    all_to_all x1, starting transfers between devices, exchange(): return lax.all_to_all(x, axis, split_axis=0, concat_axis=0, tiled=False)  6.65 us
    all_to_all x1, waiting for transfers between devices, exchange(): return lax.all_to_all(x, axis, split_axis=0, concat_axis=0, tiled=False)  3.9 us
    pallas_call x1, Pallas kernels, on_device(): pl.pallas_call(forecast_kernel, out_shape=shaped((blocks, own_rows + prio...  3.62 us
    ppermute x4, waiting for transfers between devices, swap(): return lax.ppermute(x, 'dom', [(i, i ^ distance) for i in range(count)])  3.58 us
    pallas_call x1, Pallas kernels, on_device(): pl.pallas_call(interior_kernel, out_shape=(shaped((8, slots)), shaped((ro...  3.25 us
    pallas_call x1, Pallas kernels, on_device(): pl.pallas_call(apply_kernel, out_shape=shaped((groups, own_rows, LANES)),...  1.66 us
  transfers between devices with their start and end apart: 7, of which 3 were waited for; matrix products, arithmetic and copies ran while one was open for 2% of the time, Pallas kernels for 10%

profile of v2, /device:TPU:0, one launch (start us, length us, event | category | flops | bytes accessed | tf_op | source)
XLA Modules:
  0.0 78.9 jit_solution(10279451229158741932)
XLA Ops:
  0.0 1.7 %collective-permute-start = (f32[32,128]{1,0:T(8,128)}, f32[32,128]{1,0:T(8,128)S(1)}, u32[]{:S(2)}, u32[]{:S(2)}) collective-permute-start(f32[32,128]{1,0:T(8,128)} %bitcast.15), channel_id=1, source_target_pairs={{0,2},{1,3},{2,0},{3,1},{4,6},{5,7},{6,4},{7,5},{8,10},{9,11},{10,... | collective-permute-start | bytes 49160 | tf_op jit(solution)/shard_map/ppermute | solution.py:367
  1.7 0.8 %slice_bitcast_fusion = (f32[1,5,2,256]{3,2,1,0:T(2,128)S(1)}, f32[1,5,2,256]{3,2,1,0:T(2,128)S(1)}) fusion(f32[5,32,256]{2,1,0:T(8,128)} %smooth_ref.1), kind=kLoop, calls=%fused_computation.4 | loop fusion | bytes 40960 | tf_op jit(solution)/shard_map/broadcast_in_dim | solution.py:389
  2.5 1.1 %fusion = (f32[4,5,2,256]{3,2,1,0:T(2,128)S(1)}, f32[4,5,2,256]{3,2,1,0:T(2,128)S(1)}) fusion(f32[4,5,32,256]{3,2,1,0:T(8,128)} %param.10), kind=kLoop, calls=%fused_computation.8 | loop fusion | bytes 163840 | tf_op jit(solution)/shard_map/slice | solution.py:389
  3.6 0.0 copy-start.6
  3.6 0.0 copy-start.1
  3.6 1.6 %collective-permute-start.1 = (f32[5,5,2,256]{3,2,1,0:T(2,128)S(1)}, f32[5,5,2,256]{3,2,1,0:T(2,128)S(1)}, u32[]{:S(2)}, u32[]{:S(2)}) collective-permute-start(f32[5,5,2,256]{3,2,1,0:T(2,128)S(1)} %pad_maximum_fusion.1), channel_id=1, source_target_pairs={{0,1},{1,2},{2,3},{3,4},{4,5},{5,6},{6,7},{7,8},{8,9},{9,10},{10,1... | collective-permute-start | bytes 153608 | tf_op jit(solution)/shard_map/ppermute | solution.py:390
  5.3 1.3 %collective-permute-start.2 = (f32[5,5,2,256]{3,2,1,0:T(2,128)S(1)}, f32[5,5,2,256]{3,2,1,0:T(2,128)S(1)}, u32[]{:S(2)}, u32[]{:S(2)}) collective-permute-start(f32[5,5,2,256]{3,2,1,0:T(2,128)S(1)} %pad_maximum_fusion.2), channel_id=1, source_target_pairs={{1,0},{2,1},{3,2},{4,3},{5,4},{6,5},{7,6},{8,7},{9,8},{10,9},{11,1... | collective-permute-start | bytes 153608 | tf_op jit(solution)/shard_map/ppermute | solution.py:391
  6.7 0.6 copy-done.7
  7.3 3.2 %interior.1 = (f32[8,512]{1,0:T(8,128)S(1)}, s32[32,128]{1,0:T(8,128)S(1)}, f32[4,160,256]{2,1,0:T(8,128)S(1)}, f32[20,16,256]{2,1,0:T(8,128)S(1)}, f32[5,16,256]{2,1,0:T(8,128)S(1)}) custom-call(s32[1]{0:T(128)} %bitcast.tile_ref, f32[5,5]{1,0:T(8,128)S(1)} %copy-done.7, f32[20,32,256]{2,1,0:T(8,128)} %bitcast.14, f32[5,32,256]{2,1,0:T(8,128)S(1)} %copy-done, ...), custom_call_target="tpu_custom_call" | custom-call | tf_op jit(solution)/shard_map/interior/pallas_call | solution.py:396
  10.6 5.7 %collective-permute-start.3 = (f32[64,128]{1,0:T(8,128)S(1)}, f32[64,128]{1,0:T(8,128)S(1)}, u32[]{:S(2)}, u32[]{:S(2)}) collective-permute-start(f32[64,128]{1,0:T(8,128)S(1)} %pad_maximum_fusion.3), channel_id=1, source_target_pairs={{0,4},{1,5},{2,6},{3,7},{4,0},{5,1},{6,2},{7,3},{8,12},{9,13},{10,... | collective-permute-start | bytes 98312 | tf_op jit(solution)/shard_map/ppermute | solution.py:367
  16.3 3.6 %forecast.1 = f32[8,176,128]{2,1,0:T(8,128)} custom-call(f32[5,5]{1,0:T(8,128)S(1)} %copy-done.7, f32[4,160,256]{2,1,0:T(8,128)S(1)} %get-tuple-element.18.inner_ref, f32[20,16,256]{2,1,0:T(8,128)S(1)} %get-tuple-element.19.strip_ref, f32[5,16,256]{2,1,0:T(8,128)S(1)} %get-tuple-element.20.smooth_strip_ref, ...), custom_call_target="tpu_custom_call" | custom-call | tf_op jit(solution)/shard_map/forecast/pallas_call | solution.py:426
  20.0 6.7 %all-to-all-start = ((f32[8,176,128]{2,1,0:T(8,128)}), f32[8,176,128]{2,1,0:T(8,128)S(1)}, u32[]{:S(2)}, u32[]{:S(2)}) async-start(f32[8,176,128]{2,1,0:T(8,128)} %forecast.1), calls=%async_computation | async-start | bytes 1441792 | tf_op jit(solution)/shard_map/all_to_all | solution.py:371
  26.6 3.6 %collective-permute-start.4 = (f32[128,128]{1,0:T(8,128)S(1)}, f32[128,128]{1,0:T(8,128)S(1)}, u32[]{:S(2)}, u32[]{:S(2)}) collective-permute-start(f32[128,128]{1,0:T(8,128)S(1)} %pad_maximum_fusion), channel_id=1, source_target_pairs={{0,8},{1,9},{2,10},{3,11},{4,12},{5,13},{6,14},{7,15},{8,0},{9,1},... | collective-permute-start | bytes 196616 | tf_op jit(solution)/shard_map/ppermute | solution.py:367
  30.2 2.2 %collective-permute-done.4 = f32[128,128]{1,0:T(8,128)S(1)} collective-permute-done((f32[128,128]{1,0:T(8,128)S(1)}, f32[128,128]{1,0:T(8,128)S(1)}, u32[]{:S(2)}, u32[]{:S(2)}) %collective-permute-start.4) | collective-permute-done | bytes 65568 | tf_op jit(solution)/shard_map/ppermute | solution.py:367
  32.4 1.3 %collective-permute-done.5.far_ref = f32[256,128]{1,0:T(8,128)S(1)} collective-permute-done((f32[256,128]{1,0:T(8,128)S(1)}, f32[256,128]{1,0:T(8,128)S(1)}, u32[]{:S(2)}, u32[]{:S(2)}) %collective-permute-start.5) | collective-permute-done | bytes 131104 | tf_op jit(solution)/shard_map/ppermute | solution.py:367
  33.8 0.7 localize.1.loc_ref
  34.5 3.9 %all-to-all-done.pri_ref.x_ref = f32[8,176,128]{2,1,0:T(8,128)S(1)} async-done(((f32[8,176,128]{2,1,0:T(8,128)}), f32[8,176,128]{2,1,0:T(8,128)S(1)}, u32[]{:S(2)}, u32[]{:S(2)}) %all-to-all-start) | async-done | bytes 720928 | tf_op jit(solution)/shard_map/all_to_all | solution.py:371
  38.4 0.6 first.1
  39.0 11.4 %all_to_all.20.w0_ref = f32[16,8,128]{2,1,0:T(8,128)S(1)} all-to-all(f32[16,8,128]{2,1,0:T(8,128)S(1)} %first.1), channel_id=1, replica_groups=mesh['mem'=8,'dom'=16] {'dom'}, dimensions={0} | all-to-all | bytes 131072 | tf_op jit(solution)/shard_map/all_to_all | solution.py:371
  50.4 0.9 %second.1 = f32[16,8,128]{2,1,0:T(8,128)S(1)} custom-call(s32[1]{0:T(128)} %bitcast.tile_ref, f32[16,8,128]{2,1,0:T(8,128)S(1)} %all_to_all.20.w0_ref, f32[8,176,128]{2,1,0:T(8,128)S(1)} %all-to-all-done.pri_ref.x_ref, f32[8,512]{1,0:T(8,128)S(1)} %get-tuple-element.23.params_ref, f32[2,16,256]{2,1,0:T(8,128)S(1)} %localize.1.loc_ref), custom_call_target="tpu_custom_call" | custom-call | tf_op jit(solution)/shard_map/second/pallas_call | solution.py:465
  51.3 8.7 %all_to_all.21.w1_ref = f32[16,8,128]{2,1,0:T(8,128)S(1)} all-to-all(f32[16,8,128]{2,1,0:T(8,128)S(1)} %second.1), channel_id=1, replica_groups=mesh['mem'=8,'dom'=16] {'dom'}, dimensions={0} | all-to-all | bytes 131072 | tf_op jit(solution)/shard_map/all_to_all | solution.py:371
  60.0 1.7 %apply.1 = f32[8,160,128]{2,1,0:T(8,128)S(1)} custom-call(f32[16,8,128]{2,1,0:T(8,128)S(1)} %all_to_all.20.w0_ref, f32[16,8,128]{2,1,0:T(8,128)S(1)} %all_to_all.21.w1_ref, f32[8,176,128]{2,1,0:T(8,128)S(1)} %all-to-all-done.pri_ref.x_ref), custom_call_target="tpu_custom_call" | custom-call | tf_op jit(solution)/shard_map/apply/pallas_call | solution.py:469
  61.6 16.4 %all_to_all.22 = f32[8,160,128]{2,1,0:T(8,128)S(1)} all-to-all(f32[8,160,128]{2,1,0:T(8,128)S(1)} %apply.1), channel_id=1, replica_groups=mesh['mem'=8,'dom'=16] {'mem'}, dimensions={0} | all-to-all | bytes 1310720 | tf_op jit(solution)/shard_map/all_to_all | solution.py:371
  78.0 0.9 %place.1 = f32[20,32,256]{2,1,0:T(8,128)} custom-call(f32[8,20,8,128]{3,2,1,0:T(8,128)S(1)} %bitcast.11), custom_call_target="tpu_custom_call" | custom-call | tf_op jit(solution)/shard_map/place/pallas_call | solution.py:476
  (26 shorter events, 0.1 us)
Async XLA Ops:
  0.0 10.5 %collective-permute-start = (f32[32,128]{1,0:T(8,128)}, f32[32,128]{1,0:T(8,128)S(1)}, u32[]{:S(2)}, u32[]{:S(2)}) collective-permute-start(f32[32,128]{1,0:T(8,128)} %bitcast.15), channel_id=1, source_target_pairs={{0,2},{1,3},{2,0},{3,1},{4,6},{5,7},{6,4},{7,5},{8,10},{9,11},{10,... | collective-permute-start | bytes 49160 | tf_op jit(solution)/shard_map/ppermute | solution.py:367
  2.5 4.1 %copy-start = (f32[5,32,256]{2,1,0:T(8,128)S(1)}, f32[5,32,256]{2,1,0:T(8,128)}, u32[]{:S(2)}) copy-start(f32[5,32,256]{2,1,0:T(8,128)} %smooth_ref.1) | copy-start | bytes 491524
  3.5 3.1 %copy-start.5 = (f32[2,2048]{1,0:T(2,128)S(1)}, f32[2,2048]{1,0:T(2,128)}, u32[]{:S(2)}) copy-start(f32[2,2048]{1,0:T(2,128)} %value_ref.1) | copy-start | bytes 49156
  3.6 3.1 %copy-start.6 = (f32[2,2048]{1,0:T(2,128)S(1)}, f32[2,2048]{1,0:T(2,128)}, u32[]{:S(2)}) copy-start(f32[2,2048]{1,0:T(2,128)} %error_ref.1) | copy-start | bytes 49156
  3.6 3.0 %copy-start.1 = (f32[2,2048,4]{1,2,0:T(4,128)S(1)}, f32[2,2048,4]{1,2,0:T(4,128)}, u32[]{:S(2)}) copy-start(f32[2,2048,4]{1,2,0:T(4,128)} %param.16) | copy-start | bytes 196612
  3.6 7.0 %collective-permute-start.1 = (f32[5,5,2,256]{3,2,1,0:T(2,128)S(1)}, f32[5,5,2,256]{3,2,1,0:T(2,128)S(1)}, u32[]{:S(2)}, u32[]{:S(2)}) collective-permute-start(f32[5,5,2,256]{3,2,1,0:T(2,128)S(1)} %pad_maximum_fusion.1), channel_id=1, source_target_pairs={{0,1},{1,2},{2,3},{3,4},{4,5},{5,6},{6,7},{7,8},{8,9},{9,10},{10,1... | collective-permute-start | bytes 153608 | tf_op jit(solution)/shard_map/ppermute | solution.py:390
  5.2 1.4 %copy-start.2 = (s32[2,2048,1]{1,2,0:T(1,128)S(1)}, s32[2,2048,1]{1,2,0:T(1,128)}, u32[]{:S(2)}) copy-start(s32[2,2048,1]{1,2,0:T(1,128)} %param.13) | copy-start | bytes 49156
  5.2 1.4 %copy-start.3 = (s32[2,2048]{1,0:T(2,128)S(1)}, s32[2,2048]{1,0:T(2,128)}, u32[]{:S(2)}) copy-start(s32[2,2048]{1,0:T(2,128)} %place_ref.1) | copy-start | bytes 49156
  5.2 1.4 %copy-start.4 = (s32[2,2048]{1,0:T(2,128)S(1)}, s32[2,2048]{1,0:T(2,128)}, u32[]{:S(2)}) copy-start(s32[2,2048]{1,0:T(2,128)} %field_ref.1) | copy-start | bytes 49156
  5.3 5.3 %collective-permute-start.2 = (f32[5,5,2,256]{3,2,1,0:T(2,128)S(1)}, f32[5,5,2,256]{3,2,1,0:T(2,128)S(1)}, u32[]{:S(2)}, u32[]{:S(2)}) collective-permute-start(f32[5,5,2,256]{3,2,1,0:T(2,128)S(1)} %pad_maximum_fusion.2), channel_id=1, source_target_pairs={{1,0},{2,1},{3,2},{4,3},{5,4},{6,5},{7,6},{8,7},{9,8},{10,9},{11,1... | collective-permute-start | bytes 153608 | tf_op jit(solution)/shard_map/ppermute | solution.py:391
  6.6 0.7 copy-start.7
  7.3 3.3 %copy-start.8 = (f32[2,1,2048]{2,1,0:T(1,128)S(1)}, f32[2,1,2048]{2,1,0:T(1,128)}, u32[]{:S(2)}) copy-start(f32[2,1,2048]{2,1,0:T(1,128)} %param.19) | copy-start | bytes 49156
  10.6 9.3 %collective-permute-start.3 = (f32[64,128]{1,0:T(8,128)S(1)}, f32[64,128]{1,0:T(8,128)S(1)}, u32[]{:S(2)}, u32[]{:S(2)}) collective-permute-start(f32[64,128]{1,0:T(8,128)S(1)} %pad_maximum_fusion.3), channel_id=1, source_target_pairs={{0,4},{1,5},{2,6},{3,7},{4,0},{5,1},{6,2},{7,3},{8,12},{9,13},{10,... | collective-permute-start | bytes 98312 | tf_op jit(solution)/shard_map/ppermute | solution.py:367
  20.0 18.5 %all-to-all-start = ((f32[8,176,128]{2,1,0:T(8,128)}), f32[8,176,128]{2,1,0:T(8,128)S(1)}, u32[]{:S(2)}, u32[]{:S(2)}) async-start(f32[8,176,128]{2,1,0:T(8,128)} %forecast.1), calls=%async_computation | async-start | bytes 1441792 | tf_op jit(solution)/shard_map/all_to_all | solution.py:371
  26.6 5.8 %collective-permute-start.4 = (f32[128,128]{1,0:T(8,128)S(1)}, f32[128,128]{1,0:T(8,128)S(1)}, u32[]{:S(2)}, u32[]{:S(2)}) collective-permute-start(f32[128,128]{1,0:T(8,128)S(1)} %pad_maximum_fusion), channel_id=1, source_target_pairs={{0,8},{1,9},{2,10},{3,11},{4,12},{5,13},{6,14},{7,15},{8,0},{9,1},... | collective-permute-start | bytes 196616 | tf_op jit(solution)/shard_map/ppermute | solution.py:367
  32.4 1.3 %collective-permute-start.5 = (f32[256,128]{1,0:T(8,128)S(1)}, f32[256,128]{1,0:T(8,128)S(1)}, u32[]{:S(2)}, u32[]{:S(2)}) collective-permute-start(f32[256,128]{1,0:T(8,128)S(1)} %constant_dynamic-update-slice_fusion.near_ref), channel_id=1, source_target_pairs={{0,1},{1,0},{2,3},{3,2},{4,5},{5,4},{6,7},{7,6},{8,9},{9,8},{10,11... | collective-permute-start | bytes 393224 | tf_op jit(solution)/shard_map/ppermute | solution.py:367

commit v3 on v2

--- a/solution.py
+++ b/solution.py
@@ -38,7 +38,8 @@
 
 
 def chosen_rows(slots, row):
-    return jnp.where(slots[row : row + 1, :] == iota((CAP, LANES), 0), 1.0, 0.0).astype(BF16)
+    here = slots[row : row + 1, :] == iota((CAP, LANES), 0)
+    return jnp.where(here, 1.0, 0.0).astype(BF16)
 
 
 def substep(src_ref, cross_ref, smooth, m, base):
@@ -58,6 +59,30 @@
             mixed = mixed + cross_ref[f, g] * own[g]
         result.append(v + smooth[f] * lap + mixed)
     return result
+
+
+def edge_kernel(x_ref, smooth_ref, cross_ref, tail_ref, head_ref, cross_out_ref,
+                tail_x, head_x, tail_s, head_s, sems):
+    planes, nrows, _ = x_ref.shape
+    fields = smooth_ref.shape[0]
+    top, bottom = pl.ds(0, 8), pl.ds(nrows - 8, 8)
+    copies = [
+        pltpu.make_async_copy(x_ref.at[:, bottom, :], tail_x, sems.at[0]),
+        pltpu.make_async_copy(smooth_ref.at[:, bottom, :], tail_s, sems.at[1]),
+        pltpu.make_async_copy(x_ref.at[:, top, :], head_x, sems.at[2]),
+        pltpu.make_async_copy(smooth_ref.at[:, top, :], head_s, sems.at[3]),
+        pltpu.make_async_copy(cross_ref, cross_out_ref, sems.at[4]),
+    ]
+    for copy in copies:
+        copy.start()
+    for copy in copies:
+        copy.wait()
+    for p in range(planes):
+        tail_ref[p] = tail_x[p, 6:8, :]
+        head_ref[p] = head_x[p, 0:2, :]
+    for f in range(fields):
+        tail_ref[planes + f] = tail_s[f, 6:8, :]
+        head_ref[planes + f] = head_s[f, 0:2, :]
 
 
 def interior_kernel(tile_ref, cross_ref, x_ref, smooth_ref, owner_ref, place_ref, field_ref,
@@ -91,7 +116,7 @@
                 inner_ref[m, f * nrows + 8 * g : f * nrows + 8 * g + 8, :] = v
         return carry
 
-    lax.fori_loop(0, members, member, 0)
+    lax.fori_loop(0, members, member, 0, unroll=True)
 
 
 def compact(tile_ref, owner_ref, place_ref, field_ref, weight_ref, value_ref, error_ref,
@@ -155,19 +180,18 @@
                     params_ref, out_ref, buf_ref, nxt_ref, sm_ref, fin_ref, u_ref, state_ref,
                     prior_ref, sems):
     members, points, cols = inner_ref.shape
-    _, fields, _, _ = above_ref.shape
+    fields = smooth_strip_ref.shape[0]
     nrows = points // fields
+    planes = members * fields
     fin_ref[...] = inner_ref[...]
     sm_ref[...] = smooth_strip_ref[...]
     for f in range(fields):
-        sm_ref[f, 2:3, :] = above_ref[members, f, 1:2, :]
-        sm_ref[f, 13:14, :] = below_ref[members, f, 0:1, :]
-    for m in range(members):
-        for f in range(fields):
-            p = m * fields + f
-            buf_ref[p, 8:24, :] = strip_ref[p]
-            buf_ref[p, 9:11, :] = above_ref[m, f]
-            buf_ref[p, 21:23, :] = below_ref[m, f]
+        sm_ref[f, 2:3, :] = above_ref[planes + f, 1:2, :]
+        sm_ref[f, 13:14, :] = below_ref[planes + f, 0:1, :]
+    for p in range(planes):
+        buf_ref[p, 8:24, :] = strip_ref[p]
+        buf_ref[p, 9:11, :] = above_ref[p]
+        buf_ref[p, 21:23, :] = below_ref[p]
 
     def member(m, carry):
         for h in range(2):
@@ -181,7 +205,7 @@
                 fin_ref[m, at : at + 2, :] = v[3:5]
         return carry
 
-    lax.fori_loop(0, members, member, 0)
+    lax.fori_loop(0, members, member, 0, unroll=True)
 
     halves = cols // LANES
     own_rows = members * fields * 8
@@ -231,18 +255,19 @@
     send_priors.wait()
 
 
-def load_priors(got_ref, prior_ref):
+def load_priors(got_ref, prior_ref, batch):
     groups, rows, _ = got_ref.shape
-    total, slots = prior_ref.shape
+    total = prior_ref.shape[0]
     members = total // groups
-    pieces = slots // LANES
-    first = rows - pieces * members
+    pieces = CAP // LANES
+    first = rows - (2 - batch) * pieces * members
     for s in range(groups):
         for q in range(pieces):
             k = first + q * members
             prior_ref[s * members : (s + 1) * members, q * LANES : (q + 1) * LANES] = got_ref[
                 s, k : k + members, :
             ]
+    return prior_ref[...]
 
 
 def distance(k):
@@ -261,84 +286,80 @@
     gain = (value - mean) / total - spread / (root * (jnp.sqrt(error) + root))
     gain = gain * (1.0 / (members - 1))
     groups = members // 8
-    out = jnp.zeros((tiles * 8, LANES), F32)
-    stacked = jnp.concatenate([spread] * groups, axis=0)
-    group_of = iota(stacked.shape, 0) // members
+    high, low, _ = split3(jnp.concatenate([spread] * groups, axis=0))
+    group_of = iota(high.shape, 0) // members
+    left, right = [], []
     for k in range(groups):
-        a = loc[:, None, :] * gain[None, 8 * k : 8 * k + 8, :]
-        b = jnp.where(group_of == k, stacked, 0.0)
-        out = out + dot_nt(a.reshape(tiles * 8, a.shape[2]), b, HI)
+        a = (loc[:, None, :] * gain[None, 8 * k : 8 * k + 8, :]).reshape(tiles * 8, loc.shape[1])
+        a_high, a_low, _ = split3(a)
+        b_high, b_low = [
+            jnp.where(group_of == k, p.astype(F32), 0.0).astype(BF16) for p in (high, low)
+        ]
+        left += [a_high, a_low, a_high]
+        right += [b_high, b_high, b_low]
+    out = dot_nt(jnp.concatenate(left, axis=1), jnp.concatenate(right, axis=1))
     mine = tile_ref[0]
     for k in range(tiles):
         out_ref[mine ^ distance(k)] = out[8 * k : 8 * k + 8]
 
 
-def unpack_mixing(packed_ref, members):
-    packed = jnp.sum(packed_ref[...], axis=0)
+def unpack_mixing(packed, members):
     return jnp.concatenate(
         [packed[:, k * members : (k + 1) * members] for k in range(members // 8)], axis=0
     )
 
 
 def first_kernel(tile_ref, pri_ref, params_ref, loc_ref, out_ref, prior_ref):
-    load_priors(pri_ref, prior_ref)
     value, error = params_ref[6:7, 0:CAP], params_ref[7:8, 0:CAP]
-    partial_mixing(tile_ref, out_ref, prior_ref[:, 0:CAP], value, error, loc_ref[0])
+    partial_mixing(tile_ref, out_ref, load_priors(pri_ref, prior_ref, 0), value, error, loc_ref[0])
 
 
 def second_kernel(tile_ref, w0_ref, pri_ref, params_ref, loc_ref, out_ref, prior_ref):
-    load_priors(pri_ref, prior_ref)
+    prior = load_priors(pri_ref, prior_ref, 1)
     members = prior_ref.shape[0]
-    w0 = unpack_mixing(w0_ref, members)
-    prior = prior_ref[:, CAP : 2 * CAP]
+    w0 = unpack_mixing(jnp.sum(w0_ref[...], axis=0), members)
     mean = jnp.sum(prior, axis=0, keepdims=True) * (1.0 / members)
     prior = prior + dot_nn(w0, prior - mean, HI)
     value, error = params_ref[6:7, CAP : 2 * CAP], params_ref[7:8, CAP : 2 * CAP]
     partial_mixing(tile_ref, out_ref, prior, value, error, loc_ref[1])
 
 
-def apply_kernel(w0_ref, w1_ref, x_ref, out_ref):
+def apply_kernel(w0_ref, w1_ref, got_ref, out_ref):
     groups, held, _ = out_ref.shape
-    own = 4
-    members = groups * own
+    w0_sum, w1_sum = jnp.sum(w0_ref[...], axis=0), jnp.sum(w1_ref[...], axis=0)
+    members = groups * 4
+    own = members // groups
     fields = held // (own * 8)
-    w0 = unpack_mixing(w0_ref, members)
-    w1 = unpack_mixing(w1_ref, members)
+    w0, w1 = unpack_mixing(w0_sum, members), unpack_mixing(w1_sum, members)
     inv = 1.0 / members
-    both = w0 + w1 + dot_nn(w1, w0 - jnp.sum(w0, axis=0, keepdims=True) * inv, HI)
-    both = both - jnp.sum(both, axis=1, keepdims=True) * inv
+    w = w0 + w1 + dot_nn(w1, w0 - jnp.sum(w0, axis=0, keepdims=True) * inv, HI)
+    w = w - jnp.sum(w, axis=1, keepdims=True) * inv
     size = members * 8
+    pieces = jnp.concatenate([p.astype(F32) for p in split3(w)[:2]], axis=1).astype(BF16)
     tall = jnp.where(iota((size, members), 0) // 8 == iota((size, members), 1), 1.0, 0.0)
-    wide = jnp.where(iota((members, size), 1) // 8 == iota((members, size), 0), 1.0, 0.0)
-    big = dot_nn(dot_nn(tall, both, HI), wide, HI)
-    big = jnp.where(iota((size, size), 0) % 8 == iota((size, size), 1) % 8, big, 0.0)
-    x = jnp.concatenate(
-        [
-            jnp.concatenate(
-                [
-                    x_ref[s, (m * fields + f) * 8 : (m * fields + f) * 8 + 8, :]
-                    for s in range(groups)
-                    for m in range(own)
-                ],
-                axis=0,
-            )
-            for f in range(fields)
-        ],
-        axis=1,
-    )
-    big_high, big_low, _ = split3(big)
-    x_high, x_low, _ = split3(x)
-    y = dot_nn(
-        jnp.concatenate([big_high, big_low, big_high], axis=1),
-        jnp.concatenate([x_high, x_high, x_low], axis=0),
-    )
-    y = x + y
-    for s in range(groups):
-        for m in range(own):
-            for f in range(fields):
+    wide = jnp.where(
+        iota((2 * members, 2 * size), 1) // 8 == iota((2 * members, 2 * size), 0), 1.0, 0.0
+    )
+    big = dot_nn(dot_nn(tall.astype(BF16), pieces).astype(BF16), wide.astype(BF16))
+    same = iota((size, 2 * size), 0) % 8 == iota((size, 2 * size), 1) % 8
+    big = jnp.where(same, big, 0.0).astype(BF16)
+    for f in range(fields):
+        x = jnp.concatenate(
+            [
+                got_ref[s, (m * fields + f) * 8 : (m * fields + f) * 8 + 8, :]
+                for s in range(groups)
+                for m in range(own)
+            ],
+            axis=0,
+        )
+        high, low, _ = split3(x)
+        y = dot_nn(big, jnp.concatenate([high, high], axis=0)) + dot_nn(big[:, :size], low)
+        y = x + y
+        for s in range(groups):
+            for m in range(own):
                 k = (m * fields + f) * 8
                 n = (s * own + m) * 8
-                out_ref[s, k : k + 8, :] = y[n : n + 8, f * LANES : (f + 1) * LANES]
+                out_ref[s, k : k + 8, :] = y[n : n + 8]
 
 
 def place_kernel(x_ref, out_ref, sems):
@@ -385,14 +406,35 @@
     held = loc.reshape(rows, LANES)
     held = jnp.concatenate([held, swap(held, STEPS[0])], axis=0)
 
-    tail = jnp.concatenate([x[:, :, nrows - 2 :], smooth[None, :, nrows - 2 :]], axis=0)
-    head = jnp.concatenate([x[:, :, :2], smooth[None, :, :2]], axis=0)
+    planes = members * fields
+    hbm = pl.BlockSpec(memory_space=pltpu.HBM)
+    x_hbm = pltpu.with_memory_space_constraint(x.reshape(planes, nrows, cols), pltpu.HBM)
+    tail, head, cross = pl.pallas_call(
+        edge_kernel,
+        out_shape=(
+            shaped((planes + fields, 2, cols)),
+            shaped((planes + fields, 2, cols)),
+            shaped(cross.shape),
+        ),
+        in_specs=[hbm] * 3,
+        scratch_shapes=[
+            VM((planes, 8, cols), F32),
+            VM((planes, 8, cols), F32),
+            VM((fields, 8, cols), F32),
+            VM((fields, 8, cols), F32),
+            pltpu.SemaphoreType.DMA((5,)),
+        ],
+        compiler_params=PARAMS,
+        name="edges",
+    )(
+        x_hbm,
+        pltpu.with_memory_space_constraint(smooth, pltpu.HBM),
+        pltpu.with_memory_space_constraint(cross, pltpu.HBM),
+    )
     above = lax.ppermute(tail, "dom", [(i, i + 1) for i in range(tiles - 1)])
     below = lax.ppermute(head, "dom", [(i + 1, i) for i in range(tiles - 1)])
 
     points = fields * nrows
-    planes = members * fields
-    hbm = pl.BlockSpec(memory_space=pltpu.HBM)
     params, slot, inner, strip, smooth_strip = pl.pallas_call(
         interior_kernel,
         out_shape=(
@@ -413,7 +455,7 @@
         compiler_params=PARAMS,
         name="interior",
     )(
-        mine, cross, pltpu.with_memory_space_constraint(x.reshape(planes, nrows, cols), pltpu.HBM), smooth, obs_tile.transpose(0, 2, 1), place,
+        mine, cross, x_hbm, smooth, obs_tile.transpose(0, 2, 1), place,
         field, weights.transpose(0, 2, 1), values, error,
     )
 
@@ -455,7 +497,7 @@
     total = members * groups
     mix = dict(
         out_shape=shaped((tiles, total * total // LANES, LANES)),
-        scratch_shapes=[VM((total, slots), F32)],
+        scratch_shapes=[VM((total, CAP), F32)],
         compiler_params=PARAMS,
     )
     w0 = pl.pallas_call(first_kernel, in_specs=[smem] + [vmem] * 3, name="first", **mix)(

time: 79.6 us -> 77.3 us (0.971)
  local copies, waits for them, and re-layouts: 2.54 us -> 0.05 us
    pallas_call x0 -> x1, Pallas kernels: none -> 1.15 us  [on_device(): pl.pallas_call(edge_kernel, out_shape=(shaped((planes + fields, 2, cols))...]
    slice x1 -> x0, local copies, waits for them, and re-layouts: 1.07 us -> none  [on_device(): head = jnp.concatenate([x[:, :, :2], smooth[None, :, :2]], axis=0)]
    broadcast_in_dim x1 -> x0, local copies, waits for them, and re-layouts: 0.81 us -> none  [on_device(): head = jnp.concatenate([x[:, :, :2], smooth[None, :, :2]], axis=0)]
  transfers between devices with their start and end apart: 7 -> 7, of which waited for: 3 -> 3; matrix products, arithmetic and copies ran while one was open for 2% -> 0% of each run, Pallas kernels for 10% -> 11%
where the time goes in v3:
time: 77.3 us; the launch traced here: 76.7 us
  blocking collectives  37 us (48%)
  starting transfers between devices  20.4 us (26%)
  Pallas kernels  11.5 us (15%)
  waiting for transfers between devices  7.54 us (10%)
    all_to_all x3, blocking collectives, exchange(): return lax.all_to_all(x, axis, split_axis=0, concat_axis=0, tiled=False)  37 us
    ppermute x4, starting transfers between devices, swap(): return lax.ppermute(x, 'dom', [(i, i ^ distance) for i in range(count)])  11 us
    all_to_all x1, starting transfers between devices, exchange(): return lax.all_to_all(x, axis, split_axis=0, concat_axis=0, tiled=False)  6.65 us
    all_to_all x1, waiting for transfers between devices, exchange(): return lax.all_to_all(x, axis, split_axis=0, concat_axis=0, tiled=False)  3.96 us
    ppermute x4, waiting for transfers between devices, swap(): return lax.ppermute(x, 'dom', [(i, i ^ distance) for i in range(count)])  3.58 us
    pallas_call x1, Pallas kernels, on_device(): pl.pallas_call(interior_kernel, out_shape=(shaped((8, slots)), shaped((ro...  3.23 us
    pallas_call x1, Pallas kernels, on_device(): pl.pallas_call(forecast_kernel, out_shape=shaped((blocks, own_rows + prio...  3.11 us
  transfers between devices with their start and end apart: 7, of which 3 were waited for; matrix products, arithmetic and copies ran while one was open for 0% of the time, Pallas kernels for 11%

profile of v3, /device:TPU:0, one launch (start us, length us, event | category | flops | bytes accessed | tf_op | source)
XLA Modules:
  0.0 76.7 jit_solution(15549071115071689638)
XLA Ops:
  0.0 1.7 %collective-permute-start = (f32[32,128]{1,0:T(8,128)}, f32[32,128]{1,0:T(8,128)S(1)}, u32[]{:S(2)}, u32[]{:S(2)}) collective-permute-start(f32[32,128]{1,0:T(8,128)} %bitcast.12), channel_id=1, source_target_pairs={{0,2},{1,3},{2,0},{3,1},{4,6},{5,7},{6,4},{7,5},{8,10},{9,11},{10,... | collective-permute-start | bytes 49160 | tf_op jit(solution)/shard_map/ppermute | solution.py:388
  1.7 1.1 %edges.1 = (f32[25,2,256]{2,1,0:T(2,128)S(1)}, f32[25,2,256]{2,1,0:T(2,128)S(1)}, f32[5,5]{1,0:T(8,128)S(1)}) custom-call(f32[20,32,256]{2,1,0:T(8,128)} %bitcast.10, f32[5,32,256]{2,1,0:T(8,128)} %smooth_ref.3, f32[5,5]{1,0:T(8,128)} %cross_ref.1), custom_call_target="tpu_custom_call" | custom-call | tf_op jit(solution)/shard_map/edges/pallas_call | solution.py:412
  2.8 0.0 copy-start.2
  2.9 1.5 %collective-permute-start.1 = (f32[25,2,256]{2,1,0:T(2,128)S(1)}, f32[25,2,256]{2,1,0:T(2,128)S(1)}, u32[]{:S(2)}, u32[]{:S(2)}) collective-permute-start(f32[25,2,256]{2,1,0:T(2,128)S(1)} %get-tuple-element.19), channel_id=1, source_target_pairs={{0,1},{1,2},{2,3},{3,4},{4,5},{5,6},{6,7},{7,8},{8,9},{9,10},{10,1... | collective-permute-start | bytes 153608 | tf_op jit(solution)/shard_map/ppermute | solution.py:434
  4.3 1.3 %collective-permute-start.2 = (f32[25,2,256]{2,1,0:T(2,128)S(1)}, f32[25,2,256]{2,1,0:T(2,128)S(1)}, u32[]{:S(2)}, u32[]{:S(2)}) collective-permute-start(f32[25,2,256]{2,1,0:T(2,128)S(1)} %get-tuple-element.20), channel_id=1, source_target_pairs={{1,0},{2,1},{3,2},{4,3},{5,4},{6,5},{7,6},{8,7},{9,8},{10,9},{11,1... | collective-permute-start | bytes 153608 | tf_op jit(solution)/shard_map/ppermute | solution.py:435
  5.7 0.0 copy-start.7
  5.7 3.2 %interior.1 = (f32[8,512]{1,0:T(8,128)S(1)}, s32[32,128]{1,0:T(8,128)S(1)}, f32[4,160,256]{2,1,0:T(8,128)S(1)}, f32[20,16,256]{2,1,0:T(8,128)S(1)}, f32[5,16,256]{2,1,0:T(8,128)S(1)}) custom-call(s32[1]{0:T(128)} %bitcast.tile_ref, f32[5,5]{1,0:T(8,128)S(1)} %get-tuple-element.21.cross_ref, f32[20,32,256]{2,1,0:T(8,128)} %bitcast.11, ...), custom_call_target="tpu_custom_call" | custom-call | tf_op jit(solution)/shard_map/interior/pallas_call | solution.py:438
  8.9 0.0 collective-permute-done
  9.0 0.0 collective-permute-done.1.above_ref
  9.0 5.7 %collective-permute-start.3 = (f32[64,128]{1,0:T(8,128)S(1)}, f32[64,128]{1,0:T(8,128)S(1)}, u32[]{:S(2)}, u32[]{:S(2)}) collective-permute-start(f32[64,128]{1,0:T(8,128)S(1)} %pad_maximum_fusion.1), channel_id=1, source_target_pairs={{0,4},{1,5},{2,6},{3,7},{4,0},{5,1},{6,2},{7,3},{8,12},{9,13},{10,... | collective-permute-start | bytes 98312 | tf_op jit(solution)/shard_map/ppermute | solution.py:388
  14.7 3.1 %forecast.1 = f32[8,176,128]{2,1,0:T(8,128)} custom-call(f32[5,5]{1,0:T(8,128)S(1)} %get-tuple-element.21.cross_ref, f32[4,160,256]{2,1,0:T(8,128)S(1)} %get-tuple-element.24.inner_ref, f32[20,16,256]{2,1,0:T(8,128)S(1)} %get-tuple-element.25.strip_ref, f32[5,16,256]{2,1,0:T(8,128)S(1)} %get-tuple-element.26.smooth_strip_ref, ...), custom_call_target="tpu_custom_call" | custom-call | tf_op jit(solution)/shard_map/forecast/pallas_call | solution.py:468
  17.9 6.6 %all-to-all-start = ((f32[8,176,128]{2,1,0:T(8,128)}), f32[8,176,128]{2,1,0:T(8,128)S(1)}, u32[]{:S(2)}, u32[]{:S(2)}) async-start(f32[8,176,128]{2,1,0:T(8,128)} %forecast.1), calls=%async_computation | async-start | bytes 1441792 | tf_op jit(solution)/shard_map/all_to_all | solution.py:392
  24.5 3.6 %collective-permute-start.4 = (f32[128,128]{1,0:T(8,128)S(1)}, f32[128,128]{1,0:T(8,128)S(1)}, u32[]{:S(2)}, u32[]{:S(2)}) collective-permute-start(f32[128,128]{1,0:T(8,128)S(1)} %pad_maximum_fusion), channel_id=1, source_target_pairs={{0,8},{1,9},{2,10},{3,11},{4,12},{5,13},{6,14},{7,15},{8,0},{9,1},... | collective-permute-start | bytes 196616 | tf_op jit(solution)/shard_map/ppermute | solution.py:388
  28.1 2.2 %collective-permute-done.4 = f32[128,128]{1,0:T(8,128)S(1)} collective-permute-done((f32[128,128]{1,0:T(8,128)S(1)}, f32[128,128]{1,0:T(8,128)S(1)}, u32[]{:S(2)}, u32[]{:S(2)}) %collective-permute-start.4) | collective-permute-done | bytes 65568 | tf_op jit(solution)/shard_map/ppermute | solution.py:388
  30.3 1.3 %collective-permute-done.5.far_ref = f32[256,128]{1,0:T(8,128)S(1)} collective-permute-done((f32[256,128]{1,0:T(8,128)S(1)}, f32[256,128]{1,0:T(8,128)S(1)}, u32[]{:S(2)}, u32[]{:S(2)}) %collective-permute-start.5) | collective-permute-done | bytes 131104 | tf_op jit(solution)/shard_map/ppermute | solution.py:388
  31.7 0.7 localize.1.loc_ref
  32.4 4.0 %all-to-all-done.pri_ref.got_ref = f32[8,176,128]{2,1,0:T(8,128)S(1)} async-done(((f32[8,176,128]{2,1,0:T(8,128)}), f32[8,176,128]{2,1,0:T(8,128)S(1)}, u32[]{:S(2)}, u32[]{:S(2)}) %all-to-all-start) | async-done | bytes 720928 | tf_op jit(solution)/shard_map/all_to_all | solution.py:392
  36.4 0.4 first.1
  36.8 11.9 %all_to_all.20.w0_ref = f32[16,8,128]{2,1,0:T(8,128)S(1)} all-to-all(f32[16,8,128]{2,1,0:T(8,128)S(1)} %first.1), channel_id=1, replica_groups=mesh['mem'=8,'dom'=16] {'dom'}, dimensions={0} | all-to-all | bytes 131072 | tf_op jit(solution)/shard_map/all_to_all | solution.py:392
  48.7 0.7 second.1
  49.4 8.7 %all_to_all.21.w1_ref = f32[16,8,128]{2,1,0:T(8,128)S(1)} all-to-all(f32[16,8,128]{2,1,0:T(8,128)S(1)} %second.1), channel_id=1, replica_groups=mesh['mem'=8,'dom'=16] {'dom'}, dimensions={0} | all-to-all | bytes 131072 | tf_op jit(solution)/shard_map/all_to_all | solution.py:392
  58.1 1.3 %apply.1 = f32[8,160,128]{2,1,0:T(8,128)S(1)} custom-call(f32[16,8,128]{2,1,0:T(8,128)S(1)} %all_to_all.20.w0_ref, f32[16,8,128]{2,1,0:T(8,128)S(1)} %all_to_all.21.w1_ref, f32[8,176,128]{2,1,0:T(8,128)S(1)} %all-to-all-done.pri_ref.got_ref), custom_call_target="tpu_custom_call" | custom-call | tf_op jit(solution)/shard_map/apply/pallas_call | solution.py:511
  59.4 16.4 %all_to_all.22 = f32[8,160,128]{2,1,0:T(8,128)S(1)} all-to-all(f32[8,160,128]{2,1,0:T(8,128)S(1)} %apply.1), channel_id=1, replica_groups=mesh['mem'=8,'dom'=16] {'mem'}, dimensions={0} | all-to-all | bytes 1310720 | tf_op jit(solution)/shard_map/all_to_all | solution.py:392
  75.8 0.9 %place.1 = f32[20,32,256]{2,1,0:T(8,128)} custom-call(f32[8,20,8,128]{3,2,1,0:T(8,128)S(1)} %bitcast.7), custom_call_target="tpu_custom_call" | custom-call | tf_op jit(solution)/shard_map/place/pallas_call | solution.py:518
  (21 shorter events, 0.1 us)
Async XLA Ops:
  0.0 8.9 %collective-permute-start = (f32[32,128]{1,0:T(8,128)}, f32[32,128]{1,0:T(8,128)S(1)}, u32[]{:S(2)}, u32[]{:S(2)}) collective-permute-start(f32[32,128]{1,0:T(8,128)} %bitcast.12), channel_id=1, source_target_pairs={{0,2},{1,3},{2,0},{3,1},{4,6},{5,7},{6,4},{7,5},{8,10},{9,11},{10,... | collective-permute-start | bytes 49160 | tf_op jit(solution)/shard_map/ppermute | solution.py:388
  1.7 4.0 %copy-start = (f32[5,32,256]{2,1,0:T(8,128)S(1)}, f32[5,32,256]{2,1,0:T(8,128)}, u32[]{:S(2)}) copy-start(f32[5,32,256]{2,1,0:T(8,128)} %smooth_ref.3) | copy-start | bytes 491524
  1.7 4.0 %copy-start.1 = (f32[2,2048,4]{1,2,0:T(4,128)S(1)}, f32[2,2048,4]{1,2,0:T(4,128)}, u32[]{:S(2)}) copy-start(f32[2,2048,4]{1,2,0:T(4,128)} %param.16) | copy-start | bytes 196612
  1.7 4.0 %copy-start.3 = (s32[2,2048]{1,0:T(2,128)S(1)}, s32[2,2048]{1,0:T(2,128)}, u32[]{:S(2)}) copy-start(s32[2,2048]{1,0:T(2,128)} %place_ref.1) | copy-start | bytes 49156
  1.7 4.0 %copy-start.4 = (s32[2,2048]{1,0:T(2,128)S(1)}, s32[2,2048]{1,0:T(2,128)}, u32[]{:S(2)}) copy-start(s32[2,2048]{1,0:T(2,128)} %field_ref.1) | copy-start | bytes 49156
  1.7 4.0 %copy-start.5 = (f32[2,2048]{1,0:T(2,128)S(1)}, f32[2,2048]{1,0:T(2,128)}, u32[]{:S(2)}) copy-start(f32[2,2048]{1,0:T(2,128)} %value_ref.1) | copy-start | bytes 49156
  1.7 4.0 %copy-start.6 = (f32[2,2048]{1,0:T(2,128)S(1)}, f32[2,2048]{1,0:T(2,128)}, u32[]{:S(2)}) copy-start(f32[2,2048]{1,0:T(2,128)} %error_ref.1) | copy-start | bytes 49156
  2.8 2.8 %copy-start.2 = (s32[2,2048,1]{1,2,0:T(1,128)S(1)}, s32[2,2048,1]{1,2,0:T(1,128)}, u32[]{:S(2)}) copy-start(s32[2,2048,1]{1,2,0:T(1,128)} %param.13) | copy-start | bytes 49156
  2.9 6.1 %collective-permute-start.1 = (f32[25,2,256]{2,1,0:T(2,128)S(1)}, f32[25,2,256]{2,1,0:T(2,128)S(1)}, u32[]{:S(2)}, u32[]{:S(2)}) collective-permute-start(f32[25,2,256]{2,1,0:T(2,128)S(1)} %get-tuple-element.19), channel_id=1, source_target_pairs={{0,1},{1,2},{2,3},{3,4},{4,5},{5,6},{6,7},{7,8},{8,9},{9,10},{10,1... | collective-permute-start | bytes 153608 | tf_op jit(solution)/shard_map/ppermute | solution.py:434
  4.3 4.7 %collective-permute-start.2 = (f32[25,2,256]{2,1,0:T(2,128)S(1)}, f32[25,2,256]{2,1,0:T(2,128)S(1)}, u32[]{:S(2)}, u32[]{:S(2)}) collective-permute-start(f32[25,2,256]{2,1,0:T(2,128)S(1)} %get-tuple-element.20), channel_id=1, source_target_pairs={{1,0},{2,1},{3,2},{4,3},{5,4},{6,5},{7,6},{8,7},{9,8},{10,9},{11,1... | collective-permute-start | bytes 153608 | tf_op jit(solution)/shard_map/ppermute | solution.py:435
  5.7 3.3 %copy-start.7 = (f32[2,1,2048]{2,1,0:T(1,128)S(1)}, f32[2,1,2048]{2,1,0:T(1,128)}, u32[]{:S(2)}) copy-start(f32[2,1,2048]{2,1,0:T(1,128)} %param.19) | copy-start | bytes 49156
  9.0 8.8 %collective-permute-start.3 = (f32[64,128]{1,0:T(8,128)S(1)}, f32[64,128]{1,0:T(8,128)S(1)}, u32[]{:S(2)}, u32[]{:S(2)}) collective-permute-start(f32[64,128]{1,0:T(8,128)S(1)} %pad_maximum_fusion.1), channel_id=1, source_target_pairs={{0,4},{1,5},{2,6},{3,7},{4,0},{5,1},{6,2},{7,3},{8,12},{9,13},{10,... | collective-permute-start | bytes 98312 | tf_op jit(solution)/shard_map/ppermute | solution.py:388
  17.9 18.5 %all-to-all-start = ((f32[8,176,128]{2,1,0:T(8,128)}), f32[8,176,128]{2,1,0:T(8,128)S(1)}, u32[]{:S(2)}, u32[]{:S(2)}) async-start(f32[8,176,128]{2,1,0:T(8,128)} %forecast.1), calls=%async_computation | async-start | bytes 1441792 | tf_op jit(solution)/shard_map/all_to_all | solution.py:392
  24.5 5.8 %collective-permute-start.4 = (f32[128,128]{1,0:T(8,128)S(1)}, f32[128,128]{1,0:T(8,128)S(1)}, u32[]{:S(2)}, u32[]{:S(2)}) collective-permute-start(f32[128,128]{1,0:T(8,128)S(1)} %pad_maximum_fusion), channel_id=1, source_target_pairs={{0,8},{1,9},{2,10},{3,11},{4,12},{5,13},{6,14},{7,15},{8,0},{9,1},... | collective-permute-start | bytes 196616 | tf_op jit(solution)/shard_map/ppermute | solution.py:388
  30.3 1.3 %collective-permute-start.5 = (f32[256,128]{1,0:T(8,128)S(1)}, f32[256,128]{1,0:T(8,128)S(1)}, u32[]{:S(2)}, u32[]{:S(2)}) collective-permute-start(f32[256,128]{1,0:T(8,128)S(1)} %constant_dynamic-update-slice_fusion.near_ref), channel_id=1, source_target_pairs={{0,1},{1,0},{2,3},{3,2},{4,5},{5,4},{6,7},{7,6},{8,9},{9,8},{10,11... | collective-permute-start | bytes 393224 | tf_op jit(solution)/shard_map/ppermute | solution.py:388

commit v4 on v3

--- a/solution.py
+++ b/solution.py
@@ -61,7 +61,7 @@
     return result
 
 
-def edge_kernel(x_ref, smooth_ref, cross_ref, tail_ref, head_ref, cross_out_ref,
+def edge_kernel(tile_ref, x_ref, smooth_ref, cross_ref, first_ref, second_ref, cross_out_ref,
                 tail_x, head_x, tail_s, head_s, sems):
     planes, nrows, _ = x_ref.shape
     fields = smooth_ref.shape[0]
@@ -77,12 +77,14 @@
         copy.start()
     for copy in copies:
         copy.wait()
-    for p in range(planes):
-        tail_ref[p] = tail_x[p, 6:8, :]
-        head_ref[p] = head_x[p, 0:2, :]
-    for f in range(fields):
-        tail_ref[planes + f] = tail_s[f, 6:8, :]
-        head_ref[planes + f] = head_s[f, 0:2, :]
+    even = tile_ref[0] % 2 == 0
+    for p in range(planes + fields):
+        if p < planes:
+            tail, head = tail_x[p, 6:8, :], head_x[p, 0:2, :]
+        else:
+            tail, head = tail_s[p - planes, 6:8, :], head_s[p - planes, 0:2, :]
+        first_ref[p] = jnp.where(even, tail, head)
+        second_ref[p] = jnp.where(even, head, tail)
 
 
 def interior_kernel(tile_ref, cross_ref, x_ref, smooth_ref, owner_ref, place_ref, field_ref,
@@ -176,8 +178,8 @@
 TOP = 16
 
 
-def forecast_kernel(cross_ref, inner_ref, strip_ref, smooth_strip_ref, above_ref, below_ref,
-                    params_ref, out_ref, buf_ref, nxt_ref, sm_ref, fin_ref, u_ref, state_ref,
+def forecast_kernel(tile_ref, cross_ref, inner_ref, strip_ref, smooth_strip_ref, first_ref,
+                    second_ref, params_ref, out_ref, buf_ref, nxt_ref, sm_ref, fin_ref, u_ref, state_ref,
                     prior_ref, sems):
     members, points, cols = inner_ref.shape
     fields = smooth_strip_ref.shape[0]
@@ -185,13 +187,17 @@
     planes = members * fields
     fin_ref[...] = inner_ref[...]
     sm_ref[...] = smooth_strip_ref[...]
-    for f in range(fields):
-        sm_ref[f, 2:3, :] = above_ref[planes + f, 1:2, :]
-        sm_ref[f, 13:14, :] = below_ref[planes + f, 0:1, :]
-    for p in range(planes):
-        buf_ref[p, 8:24, :] = strip_ref[p]
-        buf_ref[p, 9:11, :] = above_ref[p]
-        buf_ref[p, 21:23, :] = below_ref[p]
+    even = tile_ref[0] % 2 == 0
+    for p in range(planes + fields):
+        first, second = first_ref[p], second_ref[p]
+        above, below = jnp.where(even, second, first), jnp.where(even, first, second)
+        if p < planes:
+            buf_ref[p, 8:24, :] = strip_ref[p]
+            buf_ref[p, 9:11, :] = above
+            buf_ref[p, 21:23, :] = below
+        else:
+            sm_ref[p - planes, 2:3, :] = above[1:2]
+            sm_ref[p - planes, 13:14, :] = below[0:1]
 
     def member(m, carry):
         for h in range(2):
@@ -409,14 +415,14 @@
     planes = members * fields
     hbm = pl.BlockSpec(memory_space=pltpu.HBM)
     x_hbm = pltpu.with_memory_space_constraint(x.reshape(planes, nrows, cols), pltpu.HBM)
-    tail, head, cross = pl.pallas_call(
+    first, second, cross = pl.pallas_call(
         edge_kernel,
         out_shape=(
             shaped((planes + fields, 2, cols)),
             shaped((planes + fields, 2, cols)),
             shaped(cross.shape),
         ),
-        in_specs=[hbm] * 3,
+        in_specs=[smem] + [hbm] * 3,
         scratch_shapes=[
             VM((planes, 8, cols), F32),
             VM((planes, 8, cols), F32),
@@ -427,12 +433,14 @@
         compiler_params=PARAMS,
         name="edges",
     )(
+        mine,
         x_hbm,
         pltpu.with_memory_space_constraint(smooth, pltpu.HBM),
         pltpu.with_memory_space_constraint(cross, pltpu.HBM),
     )
-    above = lax.ppermute(tail, "dom", [(i, i + 1) for i in range(tiles - 1)])
-    below = lax.ppermute(head, "dom", [(i + 1, i) for i in range(tiles - 1)])
+    first = swap(first, 1)
+    pairs = [(i, i + 1) for i in range(1, tiles - 1, 2)]
+    second = lax.ppermute(second, "dom", pairs + [(b, a) for a, b in pairs])
 
     points = fields * nrows
     params, slot, inner, strip, smooth_strip = pl.pallas_call(
@@ -459,7 +467,7 @@
         field, weights.transpose(0, 2, 1), values, error,
     )
 
-    held, above, below, params = lax.optimization_barrier((held, above, below, params))
+    held, first, second, params = lax.optimization_barrier((held, first, second, params))
     held = jnp.concatenate([held, swap(held, STEPS[1])], axis=0)
 
     own_rows = members * fields * 8
@@ -468,7 +476,7 @@
     sent = pl.pallas_call(
         forecast_kernel,
         out_shape=shaped((blocks, own_rows + prior_rows, LANES)),
-        in_specs=[smem] + [vmem] * 6,
+        in_specs=[smem] * 2 + [vmem] * 6,
         out_specs=hbm,
         scratch_shapes=[
             VM((planes, 32, cols), F32),
@@ -482,7 +490,7 @@
         ],
         compiler_params=PARAMS,
         name="forecast",
-    )(cross, inner, strip, smooth_strip, above, below, params)
+    )(mine, cross, inner, strip, smooth_strip, first, second, params)
     held, sent = lax.optimization_barrier((held, sent))
     got = exchange(sent, "mem")
     held = jnp.concatenate([held, swap(held, STEPS[2])], axis=0)

time: 77.3 us -> 74.4 us (0.962)
  starting transfers between devices: 20.4 us -> 17 us
  waiting for transfers between devices: 7.54 us -> 9.03 us
  blocking collectives: 37 us -> 36.1 us
    ppermute x2 -> x1, starting transfers between devices: 2.75 us -> 0.66 us  [on_device(): second = lax.ppermute(second, 'dom', pairs + [(b, a) for a, b in pairs])]
    all_to_all x1, waiting for transfers between devices: 3.96 us -> 5.44 us  [exchange(): return lax.all_to_all(x, axis, split_axis=0, concat_axis=0, tiled=False)]
    ppermute x4 -> x5, starting transfers between devices: 11 us -> 9.67 us  [swap(): return lax.ppermute(x, 'dom', [(i, i ^ distance) for i in range(count)])]
    all_to_all x3, blocking collectives: 37 us -> 36.1 us  [exchange(): return lax.all_to_all(x, axis, split_axis=0, concat_axis=0, tiled=False)]
    ppermute x4 -> x5, waiting for transfers between devices: 3.58 us -> 3.58 us  [swap(): return lax.ppermute(x, 'dom', [(i, i ^ distance) for i in range(count)])]
where the time goes in v4:
time: 74.4 us; the launch traced here: 73.9 us
  blocking collectives  36.1 us (49%)
  starting transfers between devices  17 us (23%)
  Pallas kernels  11.5 us (15%)
  waiting for transfers between devices  9.03 us (12%)
    all_to_all x3, blocking collectives, exchange(): return lax.all_to_all(x, axis, split_axis=0, concat_axis=0, tiled=False)  36.1 us
    ppermute x5, starting transfers between devices, swap(): return lax.ppermute(x, 'dom', [(i, i ^ distance) for i in range(count)])  9.67 us
    all_to_all x1, starting transfers between devices, exchange(): return lax.all_to_all(x, axis, split_axis=0, concat_axis=0, tiled=False)  6.65 us
    all_to_all x1, waiting for transfers between devices, exchange(): return lax.all_to_all(x, axis, split_axis=0, concat_axis=0, tiled=False)  5.44 us
    ppermute x5, waiting for transfers between devices, swap(): return lax.ppermute(x, 'dom', [(i, i ^ distance) for i in range(count)])  3.58 us
    pallas_call x1, Pallas kernels, on_device(): pl.pallas_call(interior_kernel, out_shape=(shaped((8, slots)), shaped((ro...  3.25 us
    pallas_call x1, Pallas kernels, on_device(): pl.pallas_call(forecast_kernel, out_shape=shaped((blocks, own_rows + prio...  3.09 us
  transfers between devices with their start and end apart: 7, of which 3 were waited for; matrix products, arithmetic and copies ran while one was open for 0% of the time, Pallas kernels for 11%

profile of v4, /device:TPU:0, one launch (start us, length us, event | category | flops | bytes accessed | tf_op | source)
XLA Modules:
  0.0 73.9 jit_solution(15888032201439136554)
XLA Ops:
  0.0 1.7 %collective-permute-start = (f32[32,128]{1,0:T(8,128)}, f32[32,128]{1,0:T(8,128)S(1)}, u32[]{:S(2)}, u32[]{:S(2)}) collective-permute-start(f32[32,128]{1,0:T(8,128)} %bitcast.12), channel_id=1, source_target_pairs={{0,2},{1,3},{2,0},{3,1},{4,6},{5,7},{6,4},{7,5},{8,10},{9,11},{10,... | collective-permute-start | bytes 49160 | tf_op jit(solution)/shard_map/ppermute | solution.py:394
  1.7 1.2 %edges.1 = (f32[25,2,256]{2,1,0:T(2,128)S(1)}, f32[25,2,256]{2,1,0:T(2,128)S(1)}, f32[5,5]{1,0:T(8,128)S(1)}) custom-call(s32[1]{0:T(128)} %bitcast.tile_ref, f32[20,32,256]{2,1,0:T(8,128)} %bitcast.10, f32[5,32,256]{2,1,0:T(8,128)} %smooth_ref.3, f32[5,5]{1,0:T(8,128)} %cross_ref.1), custom_call_target="tpu_custom_call" | custom-call | tf_op jit(solution)/shard_map/edges/pallas_call | solution.py:418
  2.9 0.1 collective-permute-start.1
  3.0 0.7 collective-permute-start.2
  3.7 0.0 copy-start.7
  3.7 3.2 %interior.1 = (f32[8,512]{1,0:T(8,128)S(1)}, s32[32,128]{1,0:T(8,128)S(1)}, f32[4,160,256]{2,1,0:T(8,128)S(1)}, f32[20,16,256]{2,1,0:T(8,128)S(1)}, f32[5,16,256]{2,1,0:T(8,128)S(1)}) custom-call(s32[1]{0:T(128)} %bitcast.tile_ref, f32[5,5]{1,0:T(8,128)S(1)} %get-tuple-element.21.cross_ref, f32[20,32,256]{2,1,0:T(8,128)} %bitcast.11, ...), custom_call_target="tpu_custom_call" | custom-call | tf_op jit(solution)/shard_map/interior/pallas_call | solution.py:446
  7.0 0.0 collective-permute-done
  7.0 0.0 collective-permute-done.1.first_ref
  7.0 0.0 collective-permute-done.2.second_ref
  7.0 4.2 %collective-permute-start.3 = (f32[64,128]{1,0:T(8,128)S(1)}, f32[64,128]{1,0:T(8,128)S(1)}, u32[]{:S(2)}, u32[]{:S(2)}) collective-permute-start(f32[64,128]{1,0:T(8,128)S(1)} %pad_maximum_fusion.1), channel_id=1, source_target_pairs={{0,4},{1,5},{2,6},{3,7},{4,0},{5,1},{6,2},{7,3},{8,12},{9,13},{10,... | collective-permute-start | bytes 98312 | tf_op jit(solution)/shard_map/ppermute | solution.py:394
  11.2 3.1 %forecast.1 = f32[8,176,128]{2,1,0:T(8,128)} custom-call(s32[1]{0:T(128)} %bitcast.tile_ref, f32[5,5]{1,0:T(8,128)S(1)} %get-tuple-element.21.cross_ref, f32[4,160,256]{2,1,0:T(8,128)S(1)} %get-tuple-element.24.inner_ref, f32[20,16,256]{2,1,0:T(8,128)S(1)} %get-tuple-element.25.strip_ref, f32[5,16,256]{2,1,0:T(8,128)S(1)} %get-tuple-element.26.smooth_strip_ref, ...), custom_call_target="tpu_custom_call" | custom-call | tf_op jit(solution)/shard_map/forecast/pallas_call | solution.py:476
  14.4 6.6 %all-to-all-start = ((f32[8,176,128]{2,1,0:T(8,128)}), f32[8,176,128]{2,1,0:T(8,128)S(1)}, u32[]{:S(2)}, u32[]{:S(2)}) async-start(f32[8,176,128]{2,1,0:T(8,128)} %forecast.1), calls=%async_computation | async-start | bytes 1441792 | tf_op jit(solution)/shard_map/all_to_all | solution.py:398
  21.0 3.7 %collective-permute-start.4 = (f32[128,128]{1,0:T(8,128)S(1)}, f32[128,128]{1,0:T(8,128)S(1)}, u32[]{:S(2)}, u32[]{:S(2)}) collective-permute-start(f32[128,128]{1,0:T(8,128)S(1)} %pad_maximum_fusion), channel_id=1, source_target_pairs={{0,8},{1,9},{2,10},{3,11},{4,12},{5,13},{6,14},{7,15},{8,0},{9,1},... | collective-permute-start | bytes 196616 | tf_op jit(solution)/shard_map/ppermute | solution.py:394
  24.7 2.2 %collective-permute-done.4 = f32[128,128]{1,0:T(8,128)S(1)} collective-permute-done((f32[128,128]{1,0:T(8,128)S(1)}, f32[128,128]{1,0:T(8,128)S(1)}, u32[]{:S(2)}, u32[]{:S(2)}) %collective-permute-start.4) | collective-permute-done | bytes 65568 | tf_op jit(solution)/shard_map/ppermute | solution.py:394
  27.0 1.3 %collective-permute-done.5.far_ref = f32[256,128]{1,0:T(8,128)S(1)} collective-permute-done((f32[256,128]{1,0:T(8,128)S(1)}, f32[256,128]{1,0:T(8,128)S(1)}, u32[]{:S(2)}, u32[]{:S(2)}) %collective-permute-start.5) | collective-permute-done | bytes 131104 | tf_op jit(solution)/shard_map/ppermute | solution.py:394
  28.3 0.7 localize.1.loc_ref
  29.1 5.4 %all-to-all-done.pri_ref.got_ref = f32[8,176,128]{2,1,0:T(8,128)S(1)} async-done(((f32[8,176,128]{2,1,0:T(8,128)}), f32[8,176,128]{2,1,0:T(8,128)S(1)}, u32[]{:S(2)}, u32[]{:S(2)}) %all-to-all-start) | async-done | bytes 720928 | tf_op jit(solution)/shard_map/all_to_all | solution.py:398
  34.5 0.4 first.1
  34.9 11.1 %all_to_all.20.w0_ref = f32[16,8,128]{2,1,0:T(8,128)S(1)} all-to-all(f32[16,8,128]{2,1,0:T(8,128)S(1)} %first.1), channel_id=1, replica_groups=mesh['mem'=8,'dom'=16] {'dom'}, dimensions={0} | all-to-all | bytes 131072 | tf_op jit(solution)/shard_map/all_to_all | solution.py:398
  46.0 0.7 second.1
  46.7 8.7 %all_to_all.21.w1_ref = f32[16,8,128]{2,1,0:T(8,128)S(1)} all-to-all(f32[16,8,128]{2,1,0:T(8,128)S(1)} %second.1), channel_id=1, replica_groups=mesh['mem'=8,'dom'=16] {'dom'}, dimensions={0} | all-to-all | bytes 131072 | tf_op jit(solution)/shard_map/all_to_all | solution.py:398
  55.4 1.3 %apply.1 = f32[8,160,128]{2,1,0:T(8,128)S(1)} custom-call(f32[16,8,128]{2,1,0:T(8,128)S(1)} %all_to_all.20.w0_ref, f32[16,8,128]{2,1,0:T(8,128)S(1)} %all_to_all.21.w1_ref, f32[8,176,128]{2,1,0:T(8,128)S(1)} %all-to-all-done.pri_ref.got_ref), custom_call_target="tpu_custom_call" | custom-call | tf_op jit(solution)/shard_map/apply/pallas_call | solution.py:519
  56.7 16.4 %all_to_all.22 = f32[8,160,128]{2,1,0:T(8,128)S(1)} all-to-all(f32[8,160,128]{2,1,0:T(8,128)S(1)} %apply.1), channel_id=1, replica_groups=mesh['mem'=8,'dom'=16] {'mem'}, dimensions={0} | all-to-all | bytes 1310720 | tf_op jit(solution)/shard_map/all_to_all | solution.py:398
  73.0 0.9 %place.1 = f32[20,32,256]{2,1,0:T(8,128)} custom-call(f32[8,20,8,128]{3,2,1,0:T(8,128)S(1)} %bitcast.7), custom_call_target="tpu_custom_call" | custom-call | tf_op jit(solution)/shard_map/place/pallas_call | solution.py:526
  (21 shorter events, 0.1 us)
Async XLA Ops:
  0.0 7.0 %collective-permute-start = (f32[32,128]{1,0:T(8,128)}, f32[32,128]{1,0:T(8,128)S(1)}, u32[]{:S(2)}, u32[]{:S(2)}) collective-permute-start(f32[32,128]{1,0:T(8,128)} %bitcast.12), channel_id=1, source_target_pairs={{0,2},{1,3},{2,0},{3,1},{4,6},{5,7},{6,4},{7,5},{8,10},{9,11},{10,... | collective-permute-start | bytes 49160 | tf_op jit(solution)/shard_map/ppermute | solution.py:394
  1.7 2.0 %copy-start = (f32[5,32,256]{2,1,0:T(8,128)S(1)}, f32[5,32,256]{2,1,0:T(8,128)}, u32[]{:S(2)}) copy-start(f32[5,32,256]{2,1,0:T(8,128)} %smooth_ref.3) | copy-start | bytes 491524
  1.7 2.0 %copy-start.1 = (f32[2,2048,4]{1,2,0:T(4,128)S(1)}, f32[2,2048,4]{1,2,0:T(4,128)}, u32[]{:S(2)}) copy-start(f32[2,2048,4]{1,2,0:T(4,128)} %param.16) | copy-start | bytes 196612
  1.7 2.0 %copy-start.2 = (s32[2,2048,1]{1,2,0:T(1,128)S(1)}, s32[2,2048,1]{1,2,0:T(1,128)}, u32[]{:S(2)}) copy-start(s32[2,2048,1]{1,2,0:T(1,128)} %param.13) | copy-start | bytes 49156
  1.7 2.0 %copy-start.3 = (s32[2,2048]{1,0:T(2,128)S(1)}, s32[2,2048]{1,0:T(2,128)}, u32[]{:S(2)}) copy-start(s32[2,2048]{1,0:T(2,128)} %place_ref.1) | copy-start | bytes 49156
  1.7 2.0 %copy-start.4 = (s32[2,2048]{1,0:T(2,128)S(1)}, s32[2,2048]{1,0:T(2,128)}, u32[]{:S(2)}) copy-start(s32[2,2048]{1,0:T(2,128)} %field_ref.1) | copy-start | bytes 49156
  1.7 2.0 %copy-start.5 = (f32[2,2048]{1,0:T(2,128)S(1)}, f32[2,2048]{1,0:T(2,128)}, u32[]{:S(2)}) copy-start(f32[2,2048]{1,0:T(2,128)} %value_ref.1) | copy-start | bytes 49156
  1.7 2.0 %copy-start.6 = (f32[2,2048]{1,0:T(2,128)S(1)}, f32[2,2048]{1,0:T(2,128)}, u32[]{:S(2)}) copy-start(f32[2,2048]{1,0:T(2,128)} %error_ref.1) | copy-start | bytes 49156
  2.9 4.1 %collective-permute-start.1 = (f32[25,2,256]{2,1,0:T(2,128)S(1)}, f32[25,2,256]{2,1,0:T(2,128)S(1)}, u32[]{:S(2)}, u32[]{:S(2)}) collective-permute-start(f32[25,2,256]{2,1,0:T(2,128)S(1)} %get-tuple-element.19), channel_id=1, source_target_pairs={{0,1},{1,0},{2,3},{3,2},{4,5},{5,4},{6,7},{7,6},{8,9},{9,8},{10,11... | collective-permute-start | bytes 153608 | tf_op jit(solution)/shard_map/ppermute | solution.py:394
  3.0 4.1 %collective-permute-start.2 = (f32[25,2,256]{2,1,0:T(2,128)S(1)}, f32[25,2,256]{2,1,0:T(2,128)S(1)}, u32[]{:S(2)}, u32[]{:S(2)}) collective-permute-start(f32[25,2,256]{2,1,0:T(2,128)S(1)} %get-tuple-element.20), channel_id=1, source_target_pairs={{1,2},{3,4},{5,6},{7,8},{9,10},{11,12},{13,14},{2,1},{4,3},{6,5},{... | collective-permute-start | bytes 153608 | tf_op jit(solution)/shard_map/ppermute | solution.py:443
  3.7 3.3 %copy-start.7 = (f32[2,1,2048]{2,1,0:T(1,128)S(1)}, f32[2,1,2048]{2,1,0:T(1,128)}, u32[]{:S(2)}) copy-start(f32[2,1,2048]{2,1,0:T(1,128)} %param.19) | copy-start | bytes 49156
  7.0 7.3 %collective-permute-start.3 = (f32[64,128]{1,0:T(8,128)S(1)}, f32[64,128]{1,0:T(8,128)S(1)}, u32[]{:S(2)}, u32[]{:S(2)}) collective-permute-start(f32[64,128]{1,0:T(8,128)S(1)} %pad_maximum_fusion.1), channel_id=1, source_target_pairs={{0,4},{1,5},{2,6},{3,7},{4,0},{5,1},{6,2},{7,3},{8,12},{9,13},{10,... | collective-permute-start | bytes 98312 | tf_op jit(solution)/shard_map/ppermute | solution.py:394
  14.4 20.1 %all-to-all-start = ((f32[8,176,128]{2,1,0:T(8,128)}), f32[8,176,128]{2,1,0:T(8,128)S(1)}, u32[]{:S(2)}, u32[]{:S(2)}) async-start(f32[8,176,128]{2,1,0:T(8,128)} %forecast.1), calls=%async_computation | async-start | bytes 1441792 | tf_op jit(solution)/shard_map/all_to_all | solution.py:398
  21.0 6.0 %collective-permute-start.4 = (f32[128,128]{1,0:T(8,128)S(1)}, f32[128,128]{1,0:T(8,128)S(1)}, u32[]{:S(2)}, u32[]{:S(2)}) collective-permute-start(f32[128,128]{1,0:T(8,128)S(1)} %pad_maximum_fusion), channel_id=1, source_target_pairs={{0,8},{1,9},{2,10},{3,11},{4,12},{5,13},{6,14},{7,15},{8,0},{9,1},... | collective-permute-start | bytes 196616 | tf_op jit(solution)/shard_map/ppermute | solution.py:394
  27.0 1.3 %collective-permute-start.5 = (f32[256,128]{1,0:T(8,128)S(1)}, f32[256,128]{1,0:T(8,128)S(1)}, u32[]{:S(2)}, u32[]{:S(2)}) collective-permute-start(f32[256,128]{1,0:T(8,128)S(1)} %constant_dynamic-update-slice_fusion.near_ref), channel_id=1, source_target_pairs={{0,1},{1,0},{2,3},{3,2},{4,5},{5,4},{6,7},{7,6},{8,9},{9,8},{10,11... | collective-permute-start | bytes 393224 | tf_op jit(solution)/shard_map/ppermute | solution.py:394

commit v5 on v4

--- a/solution.py
+++ b/solution.py
@@ -10,7 +10,7 @@
 HI = lax.Precision.HIGHEST
 CAP = 256
 LANES = 128
-STEPS = (2, 4, 8, 1)
+STEPS = (8,2,4,1)
 
 
 def split3(values):
@@ -347,25 +347,36 @@
         iota((2 * members, 2 * size), 1) // 8 == iota((2 * members, 2 * size), 0), 1.0, 0.0
     )
     big = dot_nn(dot_nn(tall.astype(BF16), pieces).astype(BF16), wide.astype(BF16))
-    same = iota((size, 2 * size), 0) % 8 == iota((size, 2 * size), 1) % 8
-    big = jnp.where(same, big, 0.0).astype(BF16)
-    for f in range(fields):
+    same = (iota((size, size), 0) - iota((size, size), 1)) & 7 == 0
+    big_high, big_low = [
+        jnp.where(same, big[:, k * size : (k + 1) * size], 0.0).astype(BF16) for k in range(2)
+    ]
+    big = jnp.concatenate([big_high, big_low, big_high], axis=1)
+    for first in range(0, fields, 2):
+        pair = range(first, min(first + 2, fields))
         x = jnp.concatenate(
             [
-                got_ref[s, (m * fields + f) * 8 : (m * fields + f) * 8 + 8, :]
-                for s in range(groups)
-                for m in range(own)
+                jnp.concatenate(
+                    [
+                        got_ref[s, (m * fields + f) * 8 : (m * fields + f) * 8 + 8, :]
+                        for s in range(groups)
+                        for m in range(own)
+                    ],
+                    axis=0,
+                )
+                for f in pair
             ],
-            axis=0,
+            axis=1,
         )
         high, low, _ = split3(x)
-        y = dot_nn(big, jnp.concatenate([high, high], axis=0)) + dot_nn(big[:, :size], low)
-        y = x + y
+        y = x + dot_nn(big, jnp.concatenate([high, high, low], axis=0))
         for s in range(groups):
             for m in range(own):
-                k = (m * fields + f) * 8
-                n = (s * own + m) * 8
-                out_ref[s, k : k + 8, :] = y[n : n + 8]
+                for f in pair:
+                    k = (m * fields + f) * 8
+                    n = (s * own + m) * 8
+                    c = (f - first) * LANES
+                    out_ref[s, k : k + 8, :] = y[n : n + 8, c : c + LANES]
 
 
 def place_kernel(x_ref, out_ref, sems):

time: 74.4 us -> 74.1 us (level)
  waiting for transfers between devices: 9.03 us -> 11.9 us
  blocking collectives: 36.1 us -> 33.3 us
    all_to_all x3, blocking collectives: 36.1 us -> 33.3 us  [exchange(): return lax.all_to_all(x, axis, split_axis=0, concat_axis=0, tiled=False)]
    all_to_all x1, waiting for transfers between devices: 5.44 us -> 7.83 us  [exchange(): return lax.all_to_all(x, axis, split_axis=0, concat_axis=0, tiled=False)]
where the time goes in v5:
time: 74.1 us; the launch traced here: 73.5 us
  blocking collectives  33.3 us (45%)
  starting transfers between devices  16.6 us (22%)
  waiting for transfers between devices  11.9 us (16%)
  Pallas kernels  11.3 us (15%)
    all_to_all x3, blocking collectives, exchange(): return lax.all_to_all(x, axis, split_axis=0, concat_axis=0, tiled=False)  33.3 us
    ppermute x5, starting transfers between devices, swap(): return lax.ppermute(x, 'dom', [(i, i ^ distance) for i in range(count)])  8.99 us
    all_to_all x1, waiting for transfers between devices, exchange(): return lax.all_to_all(x, axis, split_axis=0, concat_axis=0, tiled=False)  7.83 us
    all_to_all x1, starting transfers between devices, exchange(): return lax.all_to_all(x, axis, split_axis=0, concat_axis=0, tiled=False)  6.94 us
    ppermute x5, waiting for transfers between devices, swap(): return lax.ppermute(x, 'dom', [(i, i ^ distance) for i in range(count)])  4.1 us
    pallas_call x1, Pallas kernels, on_device(): pl.pallas_call(interior_kernel, out_shape=(shaped((8, slots)), shaped((ro...  3.25 us
    pallas_call x1, Pallas kernels, on_device(): pl.pallas_call(forecast_kernel, out_shape=shaped((blocks, own_rows + prio...  3.09 us
  transfers between devices with their start and end apart: 7, of which 3 were waited for; matrix products, arithmetic and copies ran while one was open for 0% of the time, Pallas kernels for 11%

profile of v5, /device:TPU:0, one launch (start us, length us, event | category | flops | bytes accessed | tf_op | source)
XLA Modules:
  0.0 73.5 jit_solution(4918168648795405703)
XLA Ops:
  0.0 4.0 %collective-permute-start = (f32[32,128]{1,0:T(8,128)}, f32[32,128]{1,0:T(8,128)S(1)}, u32[]{:S(2)}, u32[]{:S(2)}) collective-permute-start(f32[32,128]{1,0:T(8,128)} %bitcast.12), channel_id=1, source_target_pairs={{0,8},{1,9},{2,10},{3,11},{4,12},{5,13},{6,14},{7,15},{8,0},{9,1},... | collective-permute-start | bytes 49160 | tf_op jit(solution)/shard_map/ppermute | solution.py:405
  4.0 1.2 %edges.1 = (f32[25,2,256]{2,1,0:T(2,128)S(1)}, f32[25,2,256]{2,1,0:T(2,128)S(1)}, f32[5,5]{1,0:T(8,128)S(1)}) custom-call(s32[1]{0:T(128)} %bitcast.tile_ref, f32[20,32,256]{2,1,0:T(8,128)} %bitcast.10, f32[5,32,256]{2,1,0:T(8,128)} %smooth_ref.3, f32[5,5]{1,0:T(8,128)} %cross_ref.1), custom_call_target="tpu_custom_call" | custom-call | tf_op jit(solution)/shard_map/edges/pallas_call | solution.py:429
  5.2 0.1 collective-permute-start.1
  5.3 0.7 collective-permute-start.2
  6.0 0.0 copy-start.7
  6.0 3.2 %interior.1 = (f32[8,512]{1,0:T(8,128)S(1)}, s32[32,128]{1,0:T(8,128)S(1)}, f32[4,160,256]{2,1,0:T(8,128)S(1)}, f32[20,16,256]{2,1,0:T(8,128)S(1)}, f32[5,16,256]{2,1,0:T(8,128)S(1)}) custom-call(s32[1]{0:T(128)} %bitcast.tile_ref, f32[5,5]{1,0:T(8,128)S(1)} %get-tuple-element.21.cross_ref, f32[20,32,256]{2,1,0:T(8,128)} %bitcast.11, ...), custom_call_target="tpu_custom_call" | custom-call | tf_op jit(solution)/shard_map/interior/pallas_call | solution.py:457
  9.3 0.0 collective-permute-done
  9.3 0.0 collective-permute-done.1.first_ref
  9.3 0.0 collective-permute-done.2.second_ref
  9.3 3.4 %collective-permute-start.3 = (f32[64,128]{1,0:T(8,128)S(1)}, f32[64,128]{1,0:T(8,128)S(1)}, u32[]{:S(2)}, u32[]{:S(2)}) collective-permute-start(f32[64,128]{1,0:T(8,128)S(1)} %pad_maximum_fusion.1), channel_id=1, source_target_pairs={{0,2},{1,3},{2,0},{3,1},{4,6},{5,7},{6,4},{7,5},{8,10},{9,11},{10,... | collective-permute-start | bytes 98312 | tf_op jit(solution)/shard_map/ppermute | solution.py:405
  12.8 3.1 %forecast.1 = f32[8,176,128]{2,1,0:T(8,128)} custom-call(s32[1]{0:T(128)} %bitcast.tile_ref, f32[5,5]{1,0:T(8,128)S(1)} %get-tuple-element.21.cross_ref, f32[4,160,256]{2,1,0:T(8,128)S(1)} %get-tuple-element.24.inner_ref, f32[20,16,256]{2,1,0:T(8,128)S(1)} %get-tuple-element.25.strip_ref, f32[5,16,256]{2,1,0:T(8,128)S(1)} %get-tuple-element.26.smooth_strip_ref, ...), custom_call_target="tpu_custom_call" | custom-call | tf_op jit(solution)/shard_map/forecast/pallas_call | solution.py:487
  15.9 6.9 %all-to-all-start = ((f32[8,176,128]{2,1,0:T(8,128)}), f32[8,176,128]{2,1,0:T(8,128)S(1)}, u32[]{:S(2)}, u32[]{:S(2)}) async-start(f32[8,176,128]{2,1,0:T(8,128)} %forecast.1), calls=%async_computation | async-start | bytes 1441792 | tf_op jit(solution)/shard_map/all_to_all | solution.py:409
  22.9 1.5 %collective-permute-start.4 = (f32[128,128]{1,0:T(8,128)S(1)}, f32[128,128]{1,0:T(8,128)S(1)}, u32[]{:S(2)}, u32[]{:S(2)}) collective-permute-start(f32[128,128]{1,0:T(8,128)S(1)} %pad_maximum_fusion), channel_id=1, source_target_pairs={{0,4},{1,5},{2,6},{3,7},{4,0},{5,1},{6,2},{7,3},{8,12},{9,13},{10,... | collective-permute-start | bytes 196616 | tf_op jit(solution)/shard_map/ppermute | solution.py:405
  24.4 2.8 %collective-permute-done.4 = f32[128,128]{1,0:T(8,128)S(1)} collective-permute-done((f32[128,128]{1,0:T(8,128)S(1)}, f32[128,128]{1,0:T(8,128)S(1)}, u32[]{:S(2)}, u32[]{:S(2)}) %collective-permute-start.4) | collective-permute-done | bytes 65568 | tf_op jit(solution)/shard_map/ppermute | solution.py:405
  27.1 1.3 %collective-permute-done.5.far_ref = f32[256,128]{1,0:T(8,128)S(1)} collective-permute-done((f32[256,128]{1,0:T(8,128)S(1)}, f32[256,128]{1,0:T(8,128)S(1)}, u32[]{:S(2)}, u32[]{:S(2)}) %collective-permute-start.5) | collective-permute-done | bytes 131104 | tf_op jit(solution)/shard_map/ppermute | solution.py:405
  28.5 0.7 localize.1.loc_ref
  29.2 7.8 %all-to-all-done.pri_ref.got_ref = f32[8,176,128]{2,1,0:T(8,128)S(1)} async-done(((f32[8,176,128]{2,1,0:T(8,128)}), f32[8,176,128]{2,1,0:T(8,128)S(1)}, u32[]{:S(2)}, u32[]{:S(2)}) %all-to-all-start) | async-done | bytes 720928 | tf_op jit(solution)/shard_map/all_to_all | solution.py:409
  37.0 0.4 first.1
  37.5 8.7 %all_to_all.20.w0_ref = f32[16,8,128]{2,1,0:T(8,128)S(1)} all-to-all(f32[16,8,128]{2,1,0:T(8,128)S(1)} %first.1), channel_id=1, replica_groups=mesh['mem'=8,'dom'=16] {'dom'}, dimensions={0} | all-to-all | bytes 131072 | tf_op jit(solution)/shard_map/all_to_all | solution.py:409
  46.2 0.7 second.1
  46.8 8.7 %all_to_all.21.w1_ref = f32[16,8,128]{2,1,0:T(8,128)S(1)} all-to-all(f32[16,8,128]{2,1,0:T(8,128)S(1)} %second.1), channel_id=1, replica_groups=mesh['mem'=8,'dom'=16] {'dom'}, dimensions={0} | all-to-all | bytes 131072 | tf_op jit(solution)/shard_map/all_to_all | solution.py:409
  55.6 1.1 %apply.1 = f32[8,160,128]{2,1,0:T(8,128)S(1)} custom-call(f32[16,8,128]{2,1,0:T(8,128)S(1)} %all_to_all.20.w0_ref, f32[16,8,128]{2,1,0:T(8,128)S(1)} %all_to_all.21.w1_ref, f32[8,176,128]{2,1,0:T(8,128)S(1)} %all-to-all-done.pri_ref.got_ref), custom_call_target="tpu_custom_call" | custom-call | tf_op jit(solution)/shard_map/apply/pallas_call | solution.py:530
  56.7 15.9 %all_to_all.22 = f32[8,160,128]{2,1,0:T(8,128)S(1)} all-to-all(f32[8,160,128]{2,1,0:T(8,128)S(1)} %apply.1), channel_id=1, replica_groups=mesh['mem'=8,'dom'=16] {'mem'}, dimensions={0} | all-to-all | bytes 1310720 | tf_op jit(solution)/shard_map/all_to_all | solution.py:409
  72.6 0.9 %place.1 = f32[20,32,256]{2,1,0:T(8,128)} custom-call(f32[8,20,8,128]{3,2,1,0:T(8,128)S(1)} %bitcast.7), custom_call_target="tpu_custom_call" | custom-call | tf_op jit(solution)/shard_map/place/pallas_call | solution.py:537
  (21 shorter events, 0.1 us)
Async XLA Ops:
  0.0 9.3 %collective-permute-start = (f32[32,128]{1,0:T(8,128)}, f32[32,128]{1,0:T(8,128)S(1)}, u32[]{:S(2)}, u32[]{:S(2)}) collective-permute-start(f32[32,128]{1,0:T(8,128)} %bitcast.12), channel_id=1, source_target_pairs={{0,8},{1,9},{2,10},{3,11},{4,12},{5,13},{6,14},{7,15},{8,0},{9,1},... | collective-permute-start | bytes 49160 | tf_op jit(solution)/shard_map/ppermute | solution.py:405
  4.0 2.0 %copy-start = (f32[5,32,256]{2,1,0:T(8,128)S(1)}, f32[5,32,256]{2,1,0:T(8,128)}, u32[]{:S(2)}) copy-start(f32[5,32,256]{2,1,0:T(8,128)} %smooth_ref.3) | copy-start | bytes 491524
  4.0 2.0 %copy-start.1 = (f32[2,2048,4]{1,2,0:T(4,128)S(1)}, f32[2,2048,4]{1,2,0:T(4,128)}, u32[]{:S(2)}) copy-start(f32[2,2048,4]{1,2,0:T(4,128)} %param.16) | copy-start | bytes 196612
  4.0 2.0 %copy-start.2 = (s32[2,2048,1]{1,2,0:T(1,128)S(1)}, s32[2,2048,1]{1,2,0:T(1,128)}, u32[]{:S(2)}) copy-start(s32[2,2048,1]{1,2,0:T(1,128)} %param.13) | copy-start | bytes 49156
  4.0 2.0 %copy-start.3 = (s32[2,2048]{1,0:T(2,128)S(1)}, s32[2,2048]{1,0:T(2,128)}, u32[]{:S(2)}) copy-start(s32[2,2048]{1,0:T(2,128)} %place_ref.1) | copy-start | bytes 49156
  4.0 2.0 %copy-start.4 = (s32[2,2048]{1,0:T(2,128)S(1)}, s32[2,2048]{1,0:T(2,128)}, u32[]{:S(2)}) copy-start(s32[2,2048]{1,0:T(2,128)} %field_ref.1) | copy-start | bytes 49156
  4.0 2.0 %copy-start.5 = (f32[2,2048]{1,0:T(2,128)S(1)}, f32[2,2048]{1,0:T(2,128)}, u32[]{:S(2)}) copy-start(f32[2,2048]{1,0:T(2,128)} %value_ref.1) | copy-start | bytes 49156
  4.0 2.0 %copy-start.6 = (f32[2,2048]{1,0:T(2,128)S(1)}, f32[2,2048]{1,0:T(2,128)}, u32[]{:S(2)}) copy-start(f32[2,2048]{1,0:T(2,128)} %error_ref.1) | copy-start | bytes 49156
  5.2 4.1 %collective-permute-start.1 = (f32[25,2,256]{2,1,0:T(2,128)S(1)}, f32[25,2,256]{2,1,0:T(2,128)S(1)}, u32[]{:S(2)}, u32[]{:S(2)}) collective-permute-start(f32[25,2,256]{2,1,0:T(2,128)S(1)} %get-tuple-element.19), channel_id=1, source_target_pairs={{0,1},{1,0},{2,3},{3,2},{4,5},{5,4},{6,7},{7,6},{8,9},{9,8},{10,11... | collective-permute-start | bytes 153608 | tf_op jit(solution)/shard_map/ppermute | solution.py:405
  5.3 4.1 %collective-permute-start.2 = (f32[25,2,256]{2,1,0:T(2,128)S(1)}, f32[25,2,256]{2,1,0:T(2,128)S(1)}, u32[]{:S(2)}, u32[]{:S(2)}) collective-permute-start(f32[25,2,256]{2,1,0:T(2,128)S(1)} %get-tuple-element.20), channel_id=1, source_target_pairs={{1,2},{3,4},{5,6},{7,8},{9,10},{11,12},{13,14},{2,1},{4,3},{6,5},{... | collective-permute-start | bytes 153608 | tf_op jit(solution)/shard_map/ppermute | solution.py:454
  6.0 3.3 %copy-start.7 = (f32[2,1,2048]{2,1,0:T(1,128)S(1)}, f32[2,1,2048]{2,1,0:T(1,128)}, u32[]{:S(2)}) copy-start(f32[2,1,2048]{2,1,0:T(1,128)} %param.19) | copy-start | bytes 49156
  9.3 6.5 %collective-permute-start.3 = (f32[64,128]{1,0:T(8,128)S(1)}, f32[64,128]{1,0:T(8,128)S(1)}, u32[]{:S(2)}, u32[]{:S(2)}) collective-permute-start(f32[64,128]{1,0:T(8,128)S(1)} %pad_maximum_fusion.1), channel_id=1, source_target_pairs={{0,2},{1,3},{2,0},{3,1},{4,6},{5,7},{6,4},{7,5},{8,10},{9,11},{10,... | collective-permute-start | bytes 98312 | tf_op jit(solution)/shard_map/ppermute | solution.py:405
  15.9 21.1 %all-to-all-start = ((f32[8,176,128]{2,1,0:T(8,128)}), f32[8,176,128]{2,1,0:T(8,128)S(1)}, u32[]{:S(2)}, u32[]{:S(2)}) async-start(f32[8,176,128]{2,1,0:T(8,128)} %forecast.1), calls=%async_computation | async-start | bytes 1441792 | tf_op jit(solution)/shard_map/all_to_all | solution.py:409
  22.9 4.3 %collective-permute-start.4 = (f32[128,128]{1,0:T(8,128)S(1)}, f32[128,128]{1,0:T(8,128)S(1)}, u32[]{:S(2)}, u32[]{:S(2)}) collective-permute-start(f32[128,128]{1,0:T(8,128)S(1)} %pad_maximum_fusion), channel_id=1, source_target_pairs={{0,4},{1,5},{2,6},{3,7},{4,0},{5,1},{6,2},{7,3},{8,12},{9,13},{10,... | collective-permute-start | bytes 196616 | tf_op jit(solution)/shard_map/ppermute | solution.py:405
  27.1 1.3 %collective-permute-start.5 = (f32[256,128]{1,0:T(8,128)S(1)}, f32[256,128]{1,0:T(8,128)S(1)}, u32[]{:S(2)}, u32[]{:S(2)}) collective-permute-start(f32[256,128]{1,0:T(8,128)S(1)} %constant_dynamic-update-slice_fusion.near_ref), channel_id=1, source_target_pairs={{0,1},{1,0},{2,3},{3,2},{4,5},{5,4},{6,7},{7,6},{8,9},{9,8},{10,11... | collective-permute-start | bytes 393224 | tf_op jit(solution)/shard_map/ppermute | solution.py:405

commit v6 on v5

--- a/solution.py
+++ b/solution.py
@@ -368,7 +368,9 @@
             ],
             axis=1,
         )
-        high, low, _ = split3(x)
+        total = jnp.sum(x.reshape(members, 8, x.shape[1]), axis=0) * inv
+        anomaly = x - jnp.concatenate([total] * members, axis=0)
+        high, low, _ = split3(anomaly)
         y = x + dot_nn(big, jnp.concatenate([high, high, low], axis=0))
         for s in range(groups):
             for m in range(own):

time: 74.1 us -> 74.1 us (level)
  no operation moved by 1% of the time
where the time goes in v6:
time: 74.1 us; the launch traced here: 73.5 us
  blocking collectives  33.3 us (45%)
  starting transfers between devices  16.6 us (22%)
  waiting for transfers between devices  11.9 us (16%)
  Pallas kernels  11.3 us (15%)
    all_to_all x3, blocking collectives, exchange(): return lax.all_to_all(x, axis, split_axis=0, concat_axis=0, tiled=False)  33.3 us
    ppermute x5, starting transfers between devices, swap(): return lax.ppermute(x, 'dom', [(i, i ^ distance) for i in range(count)])  8.99 us
    all_to_all x1, waiting for transfers between devices, exchange(): return lax.all_to_all(x, axis, split_axis=0, concat_axis=0, tiled=False)  7.83 us
    all_to_all x1, starting transfers between devices, exchange(): return lax.all_to_all(x, axis, split_axis=0, concat_axis=0, tiled=False)  6.94 us
    ppermute x5, waiting for transfers between devices, swap(): return lax.ppermute(x, 'dom', [(i, i ^ distance) for i in range(count)])  4.1 us
    pallas_call x1, Pallas kernels, on_device(): pl.pallas_call(interior_kernel, out_shape=(shaped((8, slots)), shaped((ro...  3.25 us
    pallas_call x1, Pallas kernels, on_device(): pl.pallas_call(forecast_kernel, out_shape=shaped((blocks, own_rows + prio...  3.09 us
  transfers between devices with their start and end apart: 7, of which 3 were waited for; matrix products, arithmetic and copies ran while one was open for 0% of the time, Pallas kernels for 11%

profile of v6, /device:TPU:0, one launch (start us, length us, event | category | flops | bytes accessed | tf_op | source)
XLA Modules:
  0.0 73.5 jit_solution(9402934832264305692)
XLA Ops:
  0.0 4.0 %collective-permute-start = (f32[32,128]{1,0:T(8,128)}, f32[32,128]{1,0:T(8,128)S(1)}, u32[]{:S(2)}, u32[]{:S(2)}) collective-permute-start(f32[32,128]{1,0:T(8,128)} %bitcast.12), channel_id=1, source_target_pairs={{0,8},{1,9},{2,10},{3,11},{4,12},{5,13},{6,14},{7,15},{8,0},{9,1},... | collective-permute-start | bytes 49160 | tf_op jit(solution)/shard_map/ppermute | solution.py:407
  4.0 1.2 %edges.1 = (f32[25,2,256]{2,1,0:T(2,128)S(1)}, f32[25,2,256]{2,1,0:T(2,128)S(1)}, f32[5,5]{1,0:T(8,128)S(1)}) custom-call(s32[1]{0:T(128)} %bitcast.tile_ref, f32[20,32,256]{2,1,0:T(8,128)} %bitcast.10, f32[5,32,256]{2,1,0:T(8,128)} %smooth_ref.3, f32[5,5]{1,0:T(8,128)} %cross_ref.1), custom_call_target="tpu_custom_call" | custom-call | tf_op jit(solution)/shard_map/edges/pallas_call | solution.py:431
  5.2 0.1 collective-permute-start.1
  5.3 0.7 collective-permute-start.2
  6.0 0.0 copy-start.7
  6.0 3.2 %interior.1 = (f32[8,512]{1,0:T(8,128)S(1)}, s32[32,128]{1,0:T(8,128)S(1)}, f32[4,160,256]{2,1,0:T(8,128)S(1)}, f32[20,16,256]{2,1,0:T(8,128)S(1)}, f32[5,16,256]{2,1,0:T(8,128)S(1)}) custom-call(s32[1]{0:T(128)} %bitcast.tile_ref, f32[5,5]{1,0:T(8,128)S(1)} %get-tuple-element.21.cross_ref, f32[20,32,256]{2,1,0:T(8,128)} %bitcast.11, ...), custom_call_target="tpu_custom_call" | custom-call | tf_op jit(solution)/shard_map/interior/pallas_call | solution.py:459
  9.3 0.0 collective-permute-done
  9.3 0.0 collective-permute-done.1.first_ref
  9.3 0.0 collective-permute-done.2.second_ref
  9.3 3.4 %collective-permute-start.3 = (f32[64,128]{1,0:T(8,128)S(1)}, f32[64,128]{1,0:T(8,128)S(1)}, u32[]{:S(2)}, u32[]{:S(2)}) collective-permute-start(f32[64,128]{1,0:T(8,128)S(1)} %pad_maximum_fusion.1), channel_id=1, source_target_pairs={{0,2},{1,3},{2,0},{3,1},{4,6},{5,7},{6,4},{7,5},{8,10},{9,11},{10,... | collective-permute-start | bytes 98312 | tf_op jit(solution)/shard_map/ppermute | solution.py:407
  12.8 3.1 %forecast.1 = f32[8,176,128]{2,1,0:T(8,128)} custom-call(s32[1]{0:T(128)} %bitcast.tile_ref, f32[5,5]{1,0:T(8,128)S(1)} %get-tuple-element.21.cross_ref, f32[4,160,256]{2,1,0:T(8,128)S(1)} %get-tuple-element.24.inner_ref, f32[20,16,256]{2,1,0:T(8,128)S(1)} %get-tuple-element.25.strip_ref, f32[5,16,256]{2,1,0:T(8,128)S(1)} %get-tuple-element.26.smooth_strip_ref, ...), custom_call_target="tpu_custom_call" | custom-call | tf_op jit(solution)/shard_map/forecast/pallas_call | solution.py:489
  15.9 6.9 %all-to-all-start = ((f32[8,176,128]{2,1,0:T(8,128)}), f32[8,176,128]{2,1,0:T(8,128)S(1)}, u32[]{:S(2)}, u32[]{:S(2)}) async-start(f32[8,176,128]{2,1,0:T(8,128)} %forecast.1), calls=%async_computation | async-start | bytes 1441792 | tf_op jit(solution)/shard_map/all_to_all | solution.py:411
  22.9 1.5 %collective-permute-start.4 = (f32[128,128]{1,0:T(8,128)S(1)}, f32[128,128]{1,0:T(8,128)S(1)}, u32[]{:S(2)}, u32[]{:S(2)}) collective-permute-start(f32[128,128]{1,0:T(8,128)S(1)} %pad_maximum_fusion), channel_id=1, source_target_pairs={{0,4},{1,5},{2,6},{3,7},{4,0},{5,1},{6,2},{7,3},{8,12},{9,13},{10,... | collective-permute-start | bytes 196616 | tf_op jit(solution)/shard_map/ppermute | solution.py:407
  24.4 2.8 %collective-permute-done.4 = f32[128,128]{1,0:T(8,128)S(1)} collective-permute-done((f32[128,128]{1,0:T(8,128)S(1)}, f32[128,128]{1,0:T(8,128)S(1)}, u32[]{:S(2)}, u32[]{:S(2)}) %collective-permute-start.4) | collective-permute-done | bytes 65568 | tf_op jit(solution)/shard_map/ppermute | solution.py:407
  27.1 1.3 %collective-permute-done.5.far_ref = f32[256,128]{1,0:T(8,128)S(1)} collective-permute-done((f32[256,128]{1,0:T(8,128)S(1)}, f32[256,128]{1,0:T(8,128)S(1)}, u32[]{:S(2)}, u32[]{:S(2)}) %collective-permute-start.5) | collective-permute-done | bytes 131104 | tf_op jit(solution)/shard_map/ppermute | solution.py:407
  28.5 0.7 localize.1.loc_ref
  29.2 7.8 %all-to-all-done.pri_ref.got_ref = f32[8,176,128]{2,1,0:T(8,128)S(1)} async-done(((f32[8,176,128]{2,1,0:T(8,128)}), f32[8,176,128]{2,1,0:T(8,128)S(1)}, u32[]{:S(2)}, u32[]{:S(2)}) %all-to-all-start) | async-done | bytes 720928 | tf_op jit(solution)/shard_map/all_to_all | solution.py:411
  37.0 0.4 first.1
  37.5 8.7 %all_to_all.20.w0_ref = f32[16,8,128]{2,1,0:T(8,128)S(1)} all-to-all(f32[16,8,128]{2,1,0:T(8,128)S(1)} %first.1), channel_id=1, replica_groups=mesh['mem'=8,'dom'=16] {'dom'}, dimensions={0} | all-to-all | bytes 131072 | tf_op jit(solution)/shard_map/all_to_all | solution.py:411
  46.2 0.7 second.1
  46.8 8.7 %all_to_all.21.w1_ref = f32[16,8,128]{2,1,0:T(8,128)S(1)} all-to-all(f32[16,8,128]{2,1,0:T(8,128)S(1)} %second.1), channel_id=1, replica_groups=mesh['mem'=8,'dom'=16] {'dom'}, dimensions={0} | all-to-all | bytes 131072 | tf_op jit(solution)/shard_map/all_to_all | solution.py:411
  55.6 1.1 %apply.1 = f32[8,160,128]{2,1,0:T(8,128)S(1)} custom-call(f32[16,8,128]{2,1,0:T(8,128)S(1)} %all_to_all.20.w0_ref, f32[16,8,128]{2,1,0:T(8,128)S(1)} %all_to_all.21.w1_ref, f32[8,176,128]{2,1,0:T(8,128)S(1)} %all-to-all-done.pri_ref.got_ref), custom_call_target="tpu_custom_call" | custom-call | tf_op jit(solution)/shard_map/apply/pallas_call | solution.py:532
  56.7 15.9 %all_to_all.22 = f32[8,160,128]{2,1,0:T(8,128)S(1)} all-to-all(f32[8,160,128]{2,1,0:T(8,128)S(1)} %apply.1), channel_id=1, replica_groups=mesh['mem'=8,'dom'=16] {'mem'}, dimensions={0} | all-to-all | bytes 1310720 | tf_op jit(solution)/shard_map/all_to_all | solution.py:411
  72.6 0.9 %place.1 = f32[20,32,256]{2,1,0:T(8,128)} custom-call(f32[8,20,8,128]{3,2,1,0:T(8,128)S(1)} %bitcast.7), custom_call_target="tpu_custom_call" | custom-call | tf_op jit(solution)/shard_map/place/pallas_call | solution.py:539
  (21 shorter events, 0.1 us)
Async XLA Ops:
  0.0 9.3 %collective-permute-start = (f32[32,128]{1,0:T(8,128)}, f32[32,128]{1,0:T(8,128)S(1)}, u32[]{:S(2)}, u32[]{:S(2)}) collective-permute-start(f32[32,128]{1,0:T(8,128)} %bitcast.12), channel_id=1, source_target_pairs={{0,8},{1,9},{2,10},{3,11},{4,12},{5,13},{6,14},{7,15},{8,0},{9,1},... | collective-permute-start | bytes 49160 | tf_op jit(solution)/shard_map/ppermute | solution.py:407
  4.0 2.0 %copy-start = (f32[5,32,256]{2,1,0:T(8,128)S(1)}, f32[5,32,256]{2,1,0:T(8,128)}, u32[]{:S(2)}) copy-start(f32[5,32,256]{2,1,0:T(8,128)} %smooth_ref.3) | copy-start | bytes 491524
  4.0 2.0 %copy-start.1 = (f32[2,2048,4]{1,2,0:T(4,128)S(1)}, f32[2,2048,4]{1,2,0:T(4,128)}, u32[]{:S(2)}) copy-start(f32[2,2048,4]{1,2,0:T(4,128)} %param.16) | copy-start | bytes 196612
  4.0 2.0 %copy-start.2 = (s32[2,2048,1]{1,2,0:T(1,128)S(1)}, s32[2,2048,1]{1,2,0:T(1,128)}, u32[]{:S(2)}) copy-start(s32[2,2048,1]{1,2,0:T(1,128)} %param.13) | copy-start | bytes 49156
  4.0 2.0 %copy-start.3 = (s32[2,2048]{1,0:T(2,128)S(1)}, s32[2,2048]{1,0:T(2,128)}, u32[]{:S(2)}) copy-start(s32[2,2048]{1,0:T(2,128)} %place_ref.1) | copy-start | bytes 49156
  4.0 2.0 %copy-start.4 = (s32[2,2048]{1,0:T(2,128)S(1)}, s32[2,2048]{1,0:T(2,128)}, u32[]{:S(2)}) copy-start(s32[2,2048]{1,0:T(2,128)} %field_ref.1) | copy-start | bytes 49156
  4.0 2.0 %copy-start.5 = (f32[2,2048]{1,0:T(2,128)S(1)}, f32[2,2048]{1,0:T(2,128)}, u32[]{:S(2)}) copy-start(f32[2,2048]{1,0:T(2,128)} %value_ref.1) | copy-start | bytes 49156
  4.0 2.0 %copy-start.6 = (f32[2,2048]{1,0:T(2,128)S(1)}, f32[2,2048]{1,0:T(2,128)}, u32[]{:S(2)}) copy-start(f32[2,2048]{1,0:T(2,128)} %error_ref.1) | copy-start | bytes 49156
  5.2 4.1 %collective-permute-start.1 = (f32[25,2,256]{2,1,0:T(2,128)S(1)}, f32[25,2,256]{2,1,0:T(2,128)S(1)}, u32[]{:S(2)}, u32[]{:S(2)}) collective-permute-start(f32[25,2,256]{2,1,0:T(2,128)S(1)} %get-tuple-element.19), channel_id=1, source_target_pairs={{0,1},{1,0},{2,3},{3,2},{4,5},{5,4},{6,7},{7,6},{8,9},{9,8},{10,11... | collective-permute-start | bytes 153608 | tf_op jit(solution)/shard_map/ppermute | solution.py:407
  5.3 4.1 %collective-permute-start.2 = (f32[25,2,256]{2,1,0:T(2,128)S(1)}, f32[25,2,256]{2,1,0:T(2,128)S(1)}, u32[]{:S(2)}, u32[]{:S(2)}) collective-permute-start(f32[25,2,256]{2,1,0:T(2,128)S(1)} %get-tuple-element.20), channel_id=1, source_target_pairs={{1,2},{3,4},{5,6},{7,8},{9,10},{11,12},{13,14},{2,1},{4,3},{6,5},{... | collective-permute-start | bytes 153608 | tf_op jit(solution)/shard_map/ppermute | solution.py:456
  6.0 3.3 %copy-start.7 = (f32[2,1,2048]{2,1,0:T(1,128)S(1)}, f32[2,1,2048]{2,1,0:T(1,128)}, u32[]{:S(2)}) copy-start(f32[2,1,2048]{2,1,0:T(1,128)} %param.19) | copy-start | bytes 49156
  9.3 6.5 %collective-permute-start.3 = (f32[64,128]{1,0:T(8,128)S(1)}, f32[64,128]{1,0:T(8,128)S(1)}, u32[]{:S(2)}, u32[]{:S(2)}) collective-permute-start(f32[64,128]{1,0:T(8,128)S(1)} %pad_maximum_fusion.1), channel_id=1, source_target_pairs={{0,2},{1,3},{2,0},{3,1},{4,6},{5,7},{6,4},{7,5},{8,10},{9,11},{10,... | collective-permute-start | bytes 98312 | tf_op jit(solution)/shard_map/ppermute | solution.py:407
  15.9 21.1 %all-to-all-start = ((f32[8,176,128]{2,1,0:T(8,128)}), f32[8,176,128]{2,1,0:T(8,128)S(1)}, u32[]{:S(2)}, u32[]{:S(2)}) async-start(f32[8,176,128]{2,1,0:T(8,128)} %forecast.1), calls=%async_computation | async-start | bytes 1441792 | tf_op jit(solution)/shard_map/all_to_all | solution.py:411
  22.9 4.3 %collective-permute-start.4 = (f32[128,128]{1,0:T(8,128)S(1)}, f32[128,128]{1,0:T(8,128)S(1)}, u32[]{:S(2)}, u32[]{:S(2)}) collective-permute-start(f32[128,128]{1,0:T(8,128)S(1)} %pad_maximum_fusion), channel_id=1, source_target_pairs={{0,4},{1,5},{2,6},{3,7},{4,0},{5,1},{6,2},{7,3},{8,12},{9,13},{10,... | collective-permute-start | bytes 196616 | tf_op jit(solution)/shard_map/ppermute | solution.py:407
  27.1 1.3 %collective-permute-start.5 = (f32[256,128]{1,0:T(8,128)S(1)}, f32[256,128]{1,0:T(8,128)S(1)}, u32[]{:S(2)}, u32[]{:S(2)}) collective-permute-start(f32[256,128]{1,0:T(8,128)S(1)} %constant_dynamic-update-slice_fusion.near_ref), channel_id=1, source_target_pairs={{0,1},{1,0},{2,3},{3,2},{4,5},{5,4},{6,7},{7,6},{8,9},{9,8},{10,11... | collective-permute-start | bytes 393224 | tf_op jit(solution)/shard_map/ppermute | solution.py:407
